TPU v7x, 128 devices: a whole 4x4x4 slice. The times are simulated.
128 devices in a mesh: wide: 32 (over z, x, core), narrow: 4 (over y).
Axes of the slice: x: 4, y: 4, z: 4, core: 2. Of those that a mesh axis runs over, the one named last changes fastest.
Arguments:
- fields: bfloat16 [24, 128, 32, 512], P(None, None, 'wide', 'narrow'), may hold values from -6 to 6
- neighbors: int32 [4, 32, 512], P(None, 'wide', 'narrow'), may hold values from 0 to 511, as said below
- cost: int32 [32, 512], P('wide', 'narrow'), may hold values from 1 to 8
- dest: int32 [32, 512], P('wide', 'narrow'), may hold values from 0 to 127, as said below
- diffusivity: bfloat16 [128, 32, 512], P(None, 'wide', 'narrow'), may hold values from 0.099609375 to 1
- operators: bfloat16 [8, 128, 128], replicated
Outputs:
- new_fields: bfloat16 [24, 128, 32, 512], P(None, None, 'wide', 'narrow')
- column_burden: float32 [128, 24, 128], P(('wide', 'narrow'))
Inputs may be any that keep to these rules, and one draw needn't show every extreme that they name: neighbors[k, r, c] lies within 2 columns of c along the row, counted cyclically over 512, and is never c. `dest`: stretch w * (narrow devices) + n is the device at index w of wide and n of narrow. Of the columns of one device, at most 2 go to one stretch, and exactly 2 go to some stretches; every stretch receives exactly 128 columns in all. Each device deals its columns, in order of rising cost, to its stretches in turn, so that the stretches' summed costs are nearly even while the grid blocks' are not.
All inputs are finite; a program needn't handle non-finite values.
Results may differ from a plain program's by a relative error of at most 0.0068.
Values may be sent and summed in bfloat16 or wider, within the bound.
No kernel may reach another device: no remote copies, remote signals or barrier semaphores. Data moves between devices by JAX's collectives and lax.ppermute only.
A program may use at most 64 MiB of HBM per device.

v0:
```python
import jax
import jax.numpy as jnp
from jax import lax
from jax.sharding import PartitionSpec as P

REACH = 2
NEIGH = 4
KMAX = 8


mixing_rate = 0.2
block_cols = 16


def padded_2(array, sides, width):
    for axis, dim in sides:
        size, length = (lax.axis_size(axis), array.shape[dim])
        up = [(i, (i + 1) % size) for i in range(size)]
        down = [(j, i) for i, j in up]
        last = lax.slice_in_dim(array, length - width, length, axis=dim)
        leading = lax.slice_in_dim(array, 0, width, axis=dim)
        before = lax.ppermute(last, axis, up)
        after = lax.ppermute(leading, axis, down)
        array = jnp.concatenate([before, array, after], axis=dim)
    return array


def level_laplace(values):
    length = values.shape[-1]
    above = jnp.concatenate([values[..., :1], values[..., : length - 1]], axis=-1)
    below = jnp.concatenate([values[..., 1:], values[..., length - 1 :]], axis=-1)
    return above + below - 2.0 * values


def physics(incoming, coefs, gains, operators):
    lead_n, slot_n, tracer_n, level_n = incoming.shape
    total_n = lead_n * slot_n
    flat_in = incoming.reshape(total_n, tracer_n, level_n)
    flat_coef = coefs.reshape(total_n, level_n)
    flat_gain = gains.reshape(total_n).astype(jnp.float32)
    steps_int = (flat_gain * (4.0 * KMAX)).astype(jnp.int32)
    order = jnp.argsort(-steps_int, stable=True)
    order_back = jnp.argsort(order)
    sorted_in = flat_in[order]
    sorted_coef = flat_coef[order]
    sorted_gain = flat_gain[order]
    sorted_steps = steps_int[order]
    block_n = total_n // block_cols

    def one_block(index, buffers):
        change_buf, burden_buf = buffers
        begin = index * block_cols
        start = lax.dynamic_slice_in_dim(sorted_in, begin, block_cols, 0)
        coef_b = lax.dynamic_slice_in_dim(sorted_coef, begin, block_cols, 0).astype(jnp.float32)
        gain_b = lax.dynamic_slice_in_dim(sorted_gain, begin, block_cols, 0)
        step_b = lax.dynamic_slice_in_dim(sorted_steps, begin, block_cols, 0)
        scale_b = gain_b[:, None, None] * coef_b[:, None, :]
        steps_full = step_b.astype(jnp.float32)[:, None, None]
        most = jnp.max(step_b)
        state = (start, jnp.zeros(start.shape, jnp.float32))
        for step_index in range(KMAX):

            def advance(carry, step_index=step_index):
                current, final = carry
                mixed = jnp.einsum(
                    "lm,cqm->cql",
                    operators[step_index],
                    current,
                    preferred_element_type=jnp.float32,
                )
                widened = mixed + scale_b * level_laplace(mixed)
                count = float(step_index + 1)
                final = jnp.where(steps_full == count, widened, final)
                current = jnp.where(steps_full >= count, widened.astype(jnp.bfloat16), current)
                return (current, final)

            state = lax.cond(most >= step_index + 1, advance, lambda carry: carry, state)
        change = state[1] - start.astype(jnp.float32)
        change_buf = lax.dynamic_update_slice_in_dim(
            change_buf, change.astype(jnp.bfloat16), begin, 0
        )
        burden_buf = lax.dynamic_update_slice_in_dim(burden_buf, jnp.sum(change, axis=-1), begin, 0)
        return (change_buf, burden_buf)

    change_sorted, burden_sorted = lax.fori_loop(
        0,
        block_n,
        one_block,
        (
            jnp.zeros((total_n, tracer_n, level_n), jnp.bfloat16),
            jnp.zeros((total_n, tracer_n), jnp.float32),
        ),
    )
    tend = change_sorted[order_back].reshape(lead_n, slot_n, tracer_n, level_n)
    burden = burden_sorted[order_back].reshape(lead_n, slot_n, tracer_n)
    return (tend, burden)


def local(fields, neighbors, cost, dest, diffusivity, operators):
    tracer_n, level_n, row_n, col_n = fields.shape
    wide_n = lax.axis_size("wide")
    narrow_n = lax.axis_size("narrow")
    stretch_n = wide_n * narrow_n
    local_cols = row_n * col_n
    capacity = 2 * local_cols // stretch_n
    row_span = col_n * narrow_n
    column = lax.axis_index("narrow") * col_n + jnp.arange(col_n, dtype=jnp.int32)
    offset = (neighbors - column[None, None, :] + REACH) % row_span - REACH
    padded = padded_2(fields, (("narrow", 3),), REACH)
    summed = (1.0 - NEIGH * mixing_rate) * fields.astype(jnp.float32)
    for shift_by in range(-REACH, REACH + 1):
        if shift_by != 0:
            weight = jnp.sum((offset == shift_by).astype(jnp.float32), axis=0)
            moved = padded[..., REACH + shift_by : REACH + shift_by + col_n].astype(jnp.float32)
            summed = summed + mixing_rate * weight * moved
    dyn = summed.astype(jnp.bfloat16)
    target = dest.reshape(local_cols)
    one_hot = (target[:, None] == jnp.arange(stretch_n, dtype=jnp.int32)[None, :]).astype(jnp.int32)
    earlier = jnp.cumsum(one_hot, axis=0) - one_hot
    placed = jnp.sum(earlier * one_hot, axis=1)
    slot_of = target * capacity + placed
    source_of = (
        jnp.full((stretch_n * capacity,), local_cols, jnp.int32)
        .at[slot_of]
        .set(jnp.arange(local_cols, dtype=jnp.int32))
    )
    gain_own = cost.reshape(local_cols).astype(jnp.float32) / (4.0 * KMAX)
    gain_cols = jnp.concatenate([gain_own, jnp.zeros((1,), jnp.float32)])
    gain_slots = gain_cols[source_of].reshape(stretch_n, capacity)
    col_major = dyn.reshape(tracer_n * level_n, local_cols).T
    coef_major = diffusivity.reshape(level_n, local_cols).T
    padded_cols = jnp.concatenate(
        [col_major, jnp.zeros((1, tracer_n * level_n), jnp.bfloat16)], axis=0
    )
    outgoing = padded_cols[source_of].reshape(stretch_n, capacity, tracer_n, level_n)
    coef_flat = jnp.concatenate([coef_major, jnp.zeros((1, level_n), jnp.bfloat16)], axis=0)
    coef_out = coef_flat[source_of].reshape(stretch_n, capacity, level_n)
    gains = gain_slots.astype(jnp.bfloat16)
    received = (
        lax.all_to_all(outgoing, ("wide", "narrow"), split_axis=0, concat_axis=0, tiled=True),
        lax.all_to_all(coef_out, ("wide", "narrow"), split_axis=0, concat_axis=0, tiled=True),
        lax.all_to_all(gains, ("wide", "narrow"), split_axis=0, concat_axis=0, tiled=True),
    )
    tend, burden = physics(received[0], received[1], received[2], operators)
    back = lax.all_to_all(tend, ("wide", "narrow"), split_axis=0, concat_axis=0, tiled=True)
    gain_recv = received[2].astype(jnp.float32)
    back_cols = back.reshape(stretch_n * capacity, tracer_n * level_n)[slot_of]
    tend_grid = back_cols.T.reshape(tracer_n, level_n, row_n, col_n)
    valid = gain_recv.reshape(-1) > 0.0
    ranked = jnp.cumsum(valid.astype(jnp.int32)) - 1
    where_to = jnp.where(valid, ranked, local_cols)
    burden_rows = (
        jnp.zeros((local_cols, tracer_n), jnp.float32)
        .at[where_to]
        .set(burden.reshape(-1, tracer_n), mode="drop")
    )
    column_burden = burden_rows.T[None]
    new_fields = (dyn.astype(jnp.float32) + tend_grid.astype(jnp.float32)).astype(jnp.bfloat16)
    return (new_fields, column_burden)


def solution(mesh):
    in_specs = (
        P(None, None, "wide", "narrow"),
        P(None, "wide", "narrow"),
        P("wide", "narrow"),
        P("wide", "narrow"),
        P(None, "wide", "narrow"),
        P(),
    )
    out_specs = (P(None, None, "wide", "narrow"), P(("wide", "narrow"), None, None))
    return jax.shard_map(local, mesh=mesh, in_specs=in_specs, out_specs=out_specs, check_vma=False)
```

profile of v0, /device:TPU:1, one launch (start us, length us, event | category | flops | bytes accessed | tf_op | source)
XLA Modules:
  0.0 287.3 jit_solution(2957197105630218006)
XLA Ops:
  3.8 1.0 scatter_custom_fusion
  4.8 1.9 gather_fusion
  7.5 11.5 %all-to-all-start = ((bf16[128,1,2]{2,1,0:T(2,128)(2,1)}), bf16[128,1,2]{2,1,0:T(2,128)(2,1)S(1)}, u32[]{:S(2)}, u32[]{:S(2)}) async-start(bf16[128,1,2]{2,1,0:T(2,128)(2,1)} %convert_element_type.238), calls=%async_computation | async-start | bytes 131072 | tf_op jit(solution)/shard_map/all_to_all | solution.py:142
  19.7 2.7 collective-permute-start.1
  23.0 1.5 gather_fusion.5
  24.4 2.3 collective-permute-done
  28.6 7.5 %all-to-all-start.2 = ((bf16[128,2,128]{2,1,0:T(2,128)(2,1)}), bf16[128,2,128]{2,1,0:T(2,128)(2,1)S(1)}, u32[]{:S(2)}, u32[]{:S(2)}) async-start(bf16[128,2,128]{2,1,0:T(2,128)(2,1)} %bitcast.46), calls=%async_computation.2 | async-start | bytes 131072 | tf_op jit(solution)/shard_map/all_to_all | solution.py:141
  36.1 2.1 add_convert_fusion.1
  38.6 1.6 gather_fusion.2
  40.2 1.5 copy.30
  41.6 4.1 %all-to-all-done.2 = bf16[128,2,128]{2,1,0:T(2,128)(2,1)S(1)} async-done(((bf16[128,2,128]{2,1,0:T(2,128)(2,1)}), bf16[128,2,128]{2,1,0:T(2,128)(2,1)S(1)}, u32[]{:S(2)}, u32[]{:S(2)}) %all-to-all-start.2) | async-done | bytes 65568 | tf_op jit(solution)/shard_map/all_to_all | solution.py:141
  45.8 6.0 %all-to-all-start.1 = ((bf16[128,2,24,128]{3,2,1,0:T(8,128)(2,1)}), bf16[128,2,24,128]{3,2,1,0:T(8,128)(2,1)}, u32[]{:S(2)}, u32[]{:S(2)}) async-start(bf16[128,2,24,128]{3,2,1,0:T(8,128)(2,1)} %bitcast.64), calls=%async_computation.1 | async-start | bytes 3145728 | tf_op jit(solution)/shard_map/all_to_all | solution.py:140
  52.2 3.2 %sort.34 = (s32[256]{0:T(256)}, s32[256]{0:T(256)S(1)}) sort(s32[256]{0:T(256)S(1)} %fusion.68, s32[256]{0:T(256)S(1)} %iota.22), dimensions={0}, to_apply=%region_7.8 | sort | flops 2048 | bytes 4096 | tf_op jit(solution)/shard_map/jit(argsort)/sort | solution.py:42
  55.3 3.2 %sort.35 = (s32[256]{0:T(256)}, s32[256]{0:T(256)S(1)}) sort(s32[256]{0:T(256)S(1)} %get-tuple-element.314, s32[256]{0:T(256)S(1)} %iota.23), dimensions={0}, to_apply=%region_28.29 | sort | flops 2048 | bytes 4096 | tf_op jit(solution)/shard_map/jit(argsort)/sort | solution.py:43
  58.5 1.9 gather_fusion.4
  60.5 1.9 gather_fusion.1
  63.3 13.0 %all-to-all-done.1 = bf16[128,2,24,128]{3,2,1,0:T(8,128)(2,1)} async-done(((bf16[128,2,24,128]{3,2,1,0:T(8,128)(2,1)}), bf16[128,2,24,128]{3,2,1,0:T(8,128)(2,1)}, u32[]{:S(2)}, u32[]{:S(2)}) %all-to-all-start.1) | async-done | bytes 1572896 | tf_op jit(solution)/shard_map/all_to_all | solution.py:140
  76.3 3.5 %gather_fusion.3 = bf16[256,24,128]{2,1,0:T(8,128)(2,1)} fusion(bf16[256,24,128]{2,1,0:T(8,128)(2,1)} %bitcast.43, s32[1024]{0:T(1024)S(1)} %pad_clamp_fusion.2), kind=kCustom, calls=%fused_computation.3 | custom fusion | bytes 3146752 | tf_op jit(solution)/shard_map/gather | solution.py:44
  80.8 166.5 %while.15 = (s32[]{:T(128)}, bf16[256,24,128]{2,1,0:T(8,128)(2,1)S(1)}, f32[256,24]{1,0:T(8,128)S(1)}, s32[256]{0:T(256)S(1)}, bf16[256,24,128]{2,1,0:T(8,128)(2...) while((s32[]{:T(128)}, ...), condition=%wide.region_27.28_spmd, body=%wide.region_8.27_spmd.sunk | while | flops 104796064 | bytes 20315756 | solution.py:85
  93.8 1.0 fusion.104
  94.8 0.9 fusion.103
  101.8 0.9 constant_dynamic-slice_fusion.2
  107.0 1.0 fusion.104
  108.1 0.9 fusion.103
  119.5 1.0 fusion.104
  120.5 0.9 fusion.103
  127.5 0.9 constant_dynamic-slice_fusion.2
  131.1 1.0 fusion.104
  132.1 0.9 fusion.103
  139.1 0.9 constant_dynamic-slice_fusion.2
  141.8 1.0 fusion.104
  142.9 0.9 fusion.103
  152.6 1.0 fusion.104
  153.6 0.9 fusion.103
  162.5 1.0 fusion.104
  163.5 0.9 fusion.103
  172.4 1.0 fusion.104
  173.4 0.9 fusion.103
  181.5 1.0 fusion.104
  182.5 0.9 fusion.103
  190.6 1.0 fusion.104
  191.6 0.9 fusion.103
  199.7 1.0 fusion.104
  200.8 0.9 fusion.103
  208.8 1.0 fusion.104
  209.9 0.9 fusion.103
  218.0 1.0 fusion.104
  219.0 0.9 fusion.103
  227.1 1.0 fusion.104
  228.1 0.9 fusion.103
  236.2 1.0 fusion.104
  237.2 0.9 fusion.103
  245.3 1.0 fusion.104
  246.4 0.9 fusion.103
  247.3 2.0 gather_fusion.7
  249.3 4.9 %all-to-all-start.3 = ((bf16[128,2,24,128]{3,2,1,0:T(8,128)(2,1)}), bf16[128,2,24,128]{3,2,1,0:T(8,128)(2,1)S(1)}, u32[]{:S(2)}, u32[]{:S(2)}) async-start(bf16[128,2,24,128]{3,2,1,0:T(8,128)(2,1)} %bitcast.135), calls=%async_computation.3 | async-start | bytes 3145728 | tf_op jit(solution)/shard_map/all_to_all | solution.py:145
  255.6 1.9 scatter_custom_fusion.1
  258.2 20.8 %all-to-all-done.3 = bf16[128,2,24,128]{3,2,1,0:T(8,128)(2,1)S(1)} async-done(((bf16[128,2,24,128]{3,2,1,0:T(8,128)(2,1)}), bf16[128,2,24,128]{3,2,1,0:T(8,128)(2,1)S(1)}, u32[]{:S(2)}, u32[]{:S(2)}) %all-to-all-start.3) | async-done | bytes 1572896 | tf_op jit(solution)/shard_map/all_to_all | solution.py:145
  279.1 1.2 copy-done.2
  280.2 1.7 copy.33
  281.9 1.0 gather_fusion.8
  283.0 1.3 convert_bitcast_fusion.1
  284.3 1.9 copy.27
  286.2 1.1 add_convert_fusion
  (423 shorter events, 79.9 us)
Async XLA Ops:
  0.6 18.4 %copy-start = (bf16[24,128,1,128]{3,1,2,0:T(8,128)(2,1)S(1)}, bf16[24,128,1,128]{3,1,2,0:T(8,128)(2,1)}, u32[]{:S(2)}) copy-start(bf16[24,128,1,128]{3,1,2,0:T(8,128)(2,1)} %param.24) | copy-start | bytes 2359300
  7.5 21.1 %all-to-all-start = ((bf16[128,1,2]{2,1,0:T(2,128)(2,1)}), bf16[128,1,2]{2,1,0:T(2,128)(2,1)S(1)}, u32[]{:S(2)}, u32[]{:S(2)}) async-start(bf16[128,1,2]{2,1,0:T(2,128)(2,1)} %convert_element_type.238), calls=%async_computation | async-start | bytes 131072 | tf_op jit(solution)/shard_map/all_to_all | solution.py:142
  19.4 3.4 %copy-start.4 = (s32[4,1,128]{2,1,0:T(1,128)S(1)}, s32[4,1,128]{2,1,0:T(1,128)}, u32[]{:S(2)}) copy-start(s32[4,1,128]{2,1,0:T(1,128)} %param.25) | copy-start | bytes 6148
  19.4 3.4 %copy-start.3 = (bf16[128,1,128]{2,0,1:T(8,128)(2,1)S(1)}, bf16[128,1,128]{2,0,1:T(8,128)(2,1)}, u32[]{:S(2)}) copy-start(bf16[128,1,128]{2,0,1:T(8,128)(2,1)} %param.28) | copy-start | bytes 98308
  19.7 7.5 %collective-permute-start.1 = (bf16[24,128,1,2]{1,0,3,2:T(8,128)(2,1)S(1)}, bf16[24,128,1,2]{1,0,3,2:T(8,128)(2,1)S(1)}, u32[]{:S(2)}, u32[]{:S(2)}) collective-permute-start(bf16[24,128,1,2]{1,0,3,2:T(8,128)(2,1)S(1)} %copy.29), channel_id=1, source_target_pairs={{1,0},{2,1},{3,2},{0,3},{5,4},{6,5},{7,6},{4,7},{9,8},{10,9},{11,1... | collective-permute-start | bytes 36872 | tf_op jit(solution)/shard_map/ppermute | solution.py:23
  22.7 4.1 %collective-permute-start = (bf16[24,128,1,2]{1,0,3,2:T(8,128)(2,1)S(1)}, bf16[24,128,1,2]{1,0,3,2:T(8,128)(2,1)S(1)}, u32[]{:S(2)}, u32[]{:S(2)}) collective-permute-start(bf16[24,128,1,2]{1,0,3,2:T(8,128)(2,1)S(1)} %copy.28), channel_id=1, source_target_pairs={{0,1},{1,2},{2,3},{3,0},{4,5},{5,6},{6,7},{7,4},{8,9},{9,10},{10,1... | collective-permute-start | bytes 36872 | tf_op jit(solution)/shard_map/ppermute | solution.py:22
  28.6 17.2 %all-to-all-start.2 = ((bf16[128,2,128]{2,1,0:T(2,128)(2,1)}), bf16[128,2,128]{2,1,0:T(2,128)(2,1)S(1)}, u32[]{:S(2)}, u32[]{:S(2)}) async-start(bf16[128,2,128]{2,1,0:T(2,128)(2,1)} %bitcast.46), calls=%async_computation.2 | async-start | bytes 131072 | tf_op jit(solution)/shard_map/all_to_all | solution.py:141
  45.8 30.6 %all-to-all-start.1 = ((bf16[128,2,24,128]{3,2,1,0:T(8,128)(2,1)}), bf16[128,2,24,128]{3,2,1,0:T(8,128)(2,1)}, u32[]{:S(2)}, u32[]{:S(2)}) async-start(bf16[128,2,24,128]{3,2,1,0:T(8,128)(2,1)} %bitcast.64), calls=%async_computation.1 | async-start | bytes 3145728 | tf_op jit(solution)/shard_map/all_to_all | solution.py:140
  79.8 0.9 copy-start.1
  249.3 29.7 %all-to-all-start.3 = ((bf16[128,2,24,128]{3,2,1,0:T(8,128)(2,1)}), bf16[128,2,24,128]{3,2,1,0:T(8,128)(2,1)S(1)}, u32[]{:S(2)}, u32[]{:S(2)}) async-start(bf16[128,2,24,128]{3,2,1,0:T(8,128)(2,1)} %bitcast.135), calls=%async_computation.3 | async-start | bytes 3145728 | tf_op jit(solution)/shard_map/all_to_all | solution.py:145
  279.1 1.2 copy-start.2
where the time goes:
time: 290 us; the launch traced here: 287 us
  loops' own time  86.7 us (30%)
  other arithmetic  68.3 us (24%)
  local copies, waits for them, and re-layouts  52.5 us (18%)
  waiting for transfers between devices  41.2 us (14%)
  starting transfers between devices  32.6 us (11%)
  matrix products  4.94 us (2%)
    another operation x1, loops' own time, physics(): lax.fori_loop(0, block_n, one_block, (jnp.zeros((total_n, tracer_n, level...  84.4 us
    all_to_all x1, waiting for transfers between devices, local(): lax.all_to_all(tend, ('wide', 'narrow'), split_axis=0, concat_axis=0, til...  20.8 us
    reduce_sum x16, other arithmetic, one_block(): jnp.sum(change, axis=-1)  16.4 us
    dynamic_update_slice x16, other arithmetic, one_block(): lax.dynamic_update_slice_in_dim(change_buf, change.astype(jnp.bfloat16),...  14.9 us
    dynamic_slice x16, local copies, waits for them, and re-layouts, one_block(): start = lax.dynamic_slice_in_dim(sorted_in, begin, block_cols, 0)  14.5 us
    all_to_all x1, waiting for transfers between devices, local(): lax.all_to_all(outgoing, ('wide', 'narrow'), split_axis=0, concat_axis=0,...  13 us
    all_to_all x1, starting transfers between devices, local(): lax.all_to_all(gains, ('wide', 'narrow'), split_axis=0, concat_axis=0, ti...  11.5 us
    broadcast_in_dim x16, other arithmetic, one_block(): steps_full = step_b.astype(jnp.float32)[:, None, None]  11.2 us
  transfers between devices with their start and end apart: 6, of which 5 were waited for; matrix products, arithmetic and copies ran while one was open for 9% of the time, Pallas kernels for 0%

commit v1 on v0

v1 whole, which is shorter than its diff:
```python
import functools

import jax
import jax.numpy as jnp
from jax import lax
from jax.experimental import pallas as pl
from jax.experimental.pallas import tpu as pltpu
from jax.sharding import PartitionSpec as P

REACH = 2
NEIGH = 4
KMAX = 8
MIX = 0.2
TRACERS = 24
LEVELS = 128
COLS = 128
GROUP = 4
SLOT = 32

F32 = jnp.float32
BF16 = jnp.bfloat16
NT = (((1,), (1,)), ((), ()))


def iota(shape, dim):
    return lax.broadcasted_iota(jnp.int32, shape, dim)


def dot(a, b):
    return jnp.dot(a, b, preferred_element_type=F32)


def split(x):
    high = x.astype(BF16)
    return high, (x - high.astype(F32)).astype(BF16)


def level_laplace(z):
    above = jnp.concatenate([z[:1], z[:-1]], axis=0)
    below = jnp.concatenate([z[1:], z[-1:]], axis=0)
    return above + below - 2.0 * z


def main_kernel(
    fields, before, after, neighbors, cost, dest, coef, operators,
    out, sent, ops, near, far, halo, dyn, burden,
):
    for s in range(KMAX):
        op = operators[s]
        ops[s, :LEVELS] = op
        ops[s, LEVELS:] = level_laplace(op.astype(F32)).astype(BF16)

    place = iota((COLS, COLS), 0)
    here = iota((COLS, COLS), 1)
    lane = iota((1, COLS), 1)
    weight = (place == here).astype(F32)
    edge = jnp.zeros((COLS, COLS), F32)
    tag = place // TRACERS
    tag = jnp.where(tag < REACH, tag - REACH, tag + (COLS - REACH))
    for k in range(NEIGH):
        offset = ((neighbors[k : k + 1, :] - lane + REACH) & (COLS - 1)) - REACH
        reads = lane + offset
        weight += (place == reads).astype(F32)
        edge += (tag == reads).astype(F32)
    near[...] = weight.astype(BF16)
    far[...] = edge
    owner = place - (place // TRACERS) * TRACERS
    rows = jnp.concatenate(
        [before[0], before[1], after[0], after[1], jnp.zeros((SLOT, LEVELS), BF16)], axis=0
    )
    halo[...] = rows.astype(F32).T.astype(BF16)

    count = cost[...]
    scale = coef[...].astype(F32) * (count.astype(F32) / (4.0 * KMAX))
    scale2 = jnp.concatenate([scale, scale], axis=1)
    count2 = jnp.concatenate([count, count], axis=1)
    burden[...] = jnp.zeros((SLOT, COLS), F32)

    def dynamics(q, carry):
        mine = jnp.where(owner == q, far[...], 0.0).astype(BF16)
        both = jnp.concatenate([fields[q], halo[...]], axis=1)
        summed = dot(both, jnp.concatenate([near[...], mine], axis=0))
        dyn[q] = (MIX * summed).astype(BF16)
        return carry

    lax.fori_loop(0, TRACERS, dynamics, 0, unroll=4)

    pairs = GROUP // 2

    def group(g, carry):
        base = g * GROUP
        first = [
            jnp.concatenate([dyn[base + 2 * p], dyn[base + 2 * p + 1]], axis=1) for p in range(pairs)
        ]
        state = list(first)
        final = [None] * pairs
        for s in range(KMAX):
            for p in range(pairs):
                both = dot(ops[s], state[p])
                widened = both[:LEVELS] + scale2 * both[LEVELS:]
                final[p] = widened if s == 0 else jnp.where(count2 > s, widened, final[p])
                state[p] = widened.astype(BF16)
        for p in range(pairs):
            start = first[p].astype(F32)
            change = final[p] - start
            total = jnp.sum(change, axis=0, keepdims=True)
            result = (start + change.astype(BF16).astype(F32)).astype(BF16)
            for i in range(2):
                q = base + 2 * p + i
                out[q] = result[:, i * COLS : (i + 1) * COLS]
                burden[pl.ds(q, 1), :] = total[:, i * COLS : (i + 1) * COLS]
        return carry

    lax.fori_loop(0, TRACERS // GROUP, group, 0)

    target = jnp.broadcast_to(dest[...], (COLS, COLS))
    same = (target.astype(F32).T == target.astype(F32)) & (place < here)
    turn = jnp.sum(same.astype(F32), axis=0, keepdims=True)
    to = (target == place).astype(F32)
    picked = jnp.concatenate([to * (turn == 0.0), to * (turn == 1.0)], axis=1).astype(BF16)
    values = burden[...] + (iota((SLOT, COLS), 0) == TRACERS).astype(F32)
    none = jnp.zeros((SLOT, COLS), BF16)
    total = jnp.zeros((COLS, COLS), F32)
    for part in split(values):
        wide = jnp.concatenate(
            [
                jnp.concatenate([part, none], axis=1),
                jnp.concatenate([none, part], axis=1),
                jnp.zeros((2 * SLOT, 2 * COLS), BF16),
            ],
            axis=0,
        )
        total += lax.dot_general(picked, wide, NT, preferred_element_type=F32)
    sent[...] = total


def order_kernel(received, out):
    values = received[...]
    place = iota((COLS, COLS), 0)
    here = iota((COLS, COLS), 1)
    flags = values.astype(BF16)
    earlier = dot((here < place).astype(BF16), flags)
    first = values[:, TRACERS : TRACERS + 1]
    second = values[:, SLOT + TRACERS : SLOT + TRACERS + 1]
    rank = earlier[:, TRACERS : TRACERS + 1] + earlier[:, SLOT + TRACERS : SLOT + TRACERS + 1]
    spot = here.astype(F32)
    chosen = jnp.concatenate(
        [
            jnp.where(spot == rank, first, 0.0),
            jnp.where(spot == rank + first, second, 0.0),
        ],
        axis=0,
    ).astype(BF16)
    turned = values.T
    rows = jnp.concatenate([turned[:SLOT], turned[SLOT : 2 * SLOT]], axis=1)
    high, low = split(rows)
    out[...] = (dot(high, chosen) + dot(low, chosen))[:TRACERS]


def local(fields, neighbors, cost, dest, diffusivity, operators):
    size = lax.axis_size("narrow")
    up = [(i, (i + 1) % size) for i in range(size)]
    down = [(j, i) for i, j in up]
    flat = fields.reshape(TRACERS, LEVELS, COLS)
    before = lax.ppermute(flat[:, :, COLS - REACH :].transpose(2, 0, 1), "narrow", up)
    after = lax.ppermute(flat[:, :, :REACH].transpose(2, 0, 1), "narrow", down)
    new, sent = pl.pallas_call(
        main_kernel,
        out_shape=(
            jax.ShapeDtypeStruct((TRACERS, LEVELS, COLS), BF16),
            jax.ShapeDtypeStruct((COLS, COLS), F32),
        ),
        in_specs=[pl.BlockSpec(memory_space=pltpu.VMEM)] * 8,
        out_specs=[pl.BlockSpec(memory_space=pltpu.VMEM)] * 2,
        scratch_shapes=[
            pltpu.VMEM((KMAX, 2 * LEVELS, LEVELS), BF16),
            pltpu.VMEM((COLS, COLS), BF16),
            pltpu.VMEM((COLS, COLS), F32),
            pltpu.VMEM((LEVELS, COLS), BF16),
            pltpu.VMEM((TRACERS, LEVELS, COLS), BF16),
            pltpu.VMEM((SLOT, COLS), F32),
        ],
        name="physics",
    )(
        flat, before, after, neighbors.reshape(NEIGH, COLS), cost, dest,
        diffusivity.reshape(LEVELS, COLS), operators,
    )
    received = lax.all_to_all(sent, ("wide", "narrow"), split_axis=0, concat_axis=0, tiled=True)
    burden = pl.pallas_call(
        order_kernel,
        out_shape=jax.ShapeDtypeStruct((TRACERS, COLS), F32),
        in_specs=[pl.BlockSpec(memory_space=pltpu.VMEM)],
        out_specs=pl.BlockSpec(memory_space=pltpu.VMEM),
        name="order",
    )(received)
    return new.reshape(fields.shape), burden[None]


def solution(mesh):
    in_specs = (
        P(None, None, "wide", "narrow"),
        P(None, "wide", "narrow"),
        P("wide", "narrow"),
        P("wide", "narrow"),
        P(None, "wide", "narrow"),
        P(),
    )
    out_specs = (P(None, None, "wide", "narrow"), P(("wide", "narrow"), None, None))
    return jax.shard_map(local, mesh=mesh, in_specs=in_specs, out_specs=out_specs, check_vma=False)
```

time: 290 us -> 45.7 us (0.16)
  loops' own time: 86.7 us -> 0 us
  other arithmetic: 68.3 us -> 0 us
  local copies, waits for them, and re-layouts: 52.5 us -> 2.15 us
  waiting for transfers between devices: 41.2 us -> 3.75 us
  starting transfers between devices: 32.6 us -> 3.62 us
  blocking collectives: 0 us -> 19.5 us
  Pallas kernels: 0 us -> 15.8 us
  matrix products: 4.94 us -> 0 us
    another operation x129 -> x0, loops' own time: 86.7 us -> none  [the longest x1 84.4 us: physics(): lax.fori_loop(0, block_n, one_block, (jnp.zeros((total_n, tracer_n, level...]
    all_to_all x4 -> x0, waiting for transfers between devices: 38.8 us -> none  [the longest x1 20.8 us: local(): lax.all_to_all(tend, ('wide', 'narrow'), split_axis=0, concat_axis=0, til...]
    all_to_all x4 -> x0, starting transfers between devices: 29.9 us -> none  [the longest x1 11.5 us: local(): lax.all_to_all(gains, ('wide', 'narrow'), split_axis=0, concat_axis=0, ti...]
    all_to_all x0 -> x1, blocking collectives: none -> 19.5 us  [local(): lax.all_to_all(sent, ('wide', 'narrow'), split_axis=0, concat_axis=0, til...]
    reduce_sum x18 -> x0, other arithmetic: 17.2 us -> none  [the longest x16 16.4 us: one_block(): jnp.sum(change, axis=-1)]
    gather x9 -> x0, local copies, waits for them, and re-layouts: 16.2 us -> none  [the longest x1 3.47 us: physics(): sorted_in = flat_in[order]]
    pallas_call x0 -> x2, Pallas kernels: none -> 15.8 us  [the longest x1 13.9 us: local(): pl.pallas_call(main_kernel, out_shape=(jax.ShapeDtypeStruct((TRACERS, LEV...]
    dynamic_slice x32 -> x0, local copies, waits for them, and re-layouts: 15.7 us -> none  [the longest x16 14.5 us: one_block(): start = lax.dynamic_slice_in_dim(sorted_in, begin, block_cols, 0)]
  transfers between devices with their start and end apart: 6 -> 2, of which waited for: 5 -> 2; matrix products, arithmetic and copies ran while one was open for 9% -> 0% of each run, Pallas kernels for 0% -> 0%
where the time goes in v1:
time: 45.7 us; the launch traced here: 45.5 us
  blocking collectives  19.5 us (43%)
  Pallas kernels  15.8 us (35%)
  waiting for transfers between devices  3.75 us (8%)
  starting transfers between devices  3.62 us (8%)
  local copies, waits for them, and re-layouts  2.15 us (5%)
  between operations  0.65 us (1%)
    all_to_all x1, blocking collectives, local(): lax.all_to_all(sent, ('wide', 'narrow'), split_axis=0, concat_axis=0, til...  19.5 us
    pallas_call x1, Pallas kernels, local(): pl.pallas_call(main_kernel, out_shape=(jax.ShapeDtypeStruct((TRACERS, LEV...  13.9 us
    ppermute x1, starting transfers between devices, local(): after = lax.ppermute(flat[:, :, :REACH].transpose(2, 0, 1), 'narrow', down)  3.62 us
    ppermute x1, waiting for transfers between devices, local(): lax.ppermute(flat[:, :, COLS - REACH:].transpose(2, 0, 1), 'narrow', up)  2.92 us
    unnamed x5, local copies, waits for them, and re-layouts  2.14 us
    pallas_call x1, Pallas kernels, local(): pl.pallas_call(order_kernel, out_shape=jax.ShapeDtypeStruct((TRACERS, COL...  1.91 us
  transfers between devices with their start and end apart: 2, of which 2 were waited for; matrix products, arithmetic and copies ran while one was open for 0% of the time, Pallas kernels for 0%

profile of v1, /device:TPU:1, one launch (start us, length us, event | category | flops | bytes accessed | tf_op | source)
XLA Modules:
  0.0 45.5 jit_solution(5994015348777127400)
XLA Ops:
  0.6 1.5 %copy.11 = bf16[24,128,1,128]{1,0,3,2:T(8,128)(2,1)S(1)} copy(bf16[24,128,1,128]{3,1,2,0:T(8,128)(2,1)} %param.6) | data formatting | bytes 1572864 | tf_op args[0]
  2.2 3.6 %collective-permute-start.1 = (bf16[2,24,128]{2,1,0:T(8,128)(2,1)S(1)}, bf16[2,24,128]{2,1,0:T(8,128)(2,1)S(1)}, u32[]{:S(2)}, u32[]{:S(2)}) collective-permute-start(bf16[2,24,128]{2,1,0:T(8,128)(2,1)S(1)} %get-tuple-element.10), channel_id=1, source_target_pairs={{1,0},{2,1},{3,2},{0,3},{5,4},{6,5},{7,6},{4,7},{9,8},{10,9},{11,1... | collective-permute-start | bytes 36872 | tf_op jit(solution)/shard_map/ppermute | solution.py:166
  5.8 0.0 collective-permute-start
  5.8 0.8 %collective-permute-done.1.after = bf16[2,24,128]{2,1,0:T(8,128)(2,1)S(1)} collective-permute-done((bf16[2,24,128]{2,1,0:T(8,128)(2,1)S(1)}, bf16[2,24,128]{2,1,0:T(8,128)(2,1)S(1)}, u32[]{:S(2)}, u32[]{:S(2)}) %collective-permute-start.1) | collective-permute-done | bytes 12320 | tf_op jit(solution)/shard_map/ppermute | solution.py:166
  6.6 0.0 copy-start
  6.6 2.9 %collective-permute-done.before = bf16[2,24,128]{2,1,0:T(8,128)(2,1)S(1)} collective-permute-done((bf16[2,24,128]{2,1,0:T(8,128)(2,1)S(1)}, bf16[2,24,128]{2,1,0:T(8,128)(2,1)S(1)}, u32[]{:S(2)}, u32[]{:S(2)}) %collective-permute-start) | collective-permute-done | bytes 12320 | tf_op jit(solution)/shard_map/ppermute | solution.py:165
  9.6 0.0 copy-start.1
  9.6 0.0 copy-done
  9.6 0.6 %copy-done.1 = bf16[2,24,128]{2,1,0:T(8,128)(2,1)} copy-done((bf16[2,24,128]{2,1,0:T(8,128)(2,1)}, bf16[2,24,128]{2,1,0:T(8,128)(2,1)S(1)}, u32[]{:S(2)}) %copy-start.1) | copy-done | bytes 12312
  10.2 13.9 %physics.1 = (bf16[24,128,128]{2,1,0:T(8,128)(2,1)}, f32[128,128]{1,0:T(8,128)}) custom-call(bf16[24,128,128]{2,1,0:T(8,128)(2,1)} %bitcast.16, bf16[2,24,128]{2,1,0:T(8,128)(2,1)} %copy-done.1, bf16[2,24,128]{2,1,0:T(8,128)(2,1)} %copy-done, s32[4,128]{1,0:T(4,128)} %bitcast.22, s32[1,128]{1,0:T(1,128)} %cost.1, s32[1,128]{1,0:T(1,128)} %dest.1, ...), custom_call_target="tpu_custom_call" | custom-call | tf_op jit(solution)/shard_map/physics/pallas_call | solution.py:167
  24.1 19.5 %all_to_all.11 = f32[128,1,128]{2,1,0:T(1,128)} all-to-all(f32[128,1,128]{2,1,0:T(1,128)} %bitcast.19), channel_id=1, replica_groups=mesh['wide'=32,'narrow'=4] {'wide','narrow'}, dimensions={0} | all-to-all | bytes 131072 | tf_op jit(solution)/shard_map/all_to_all | solution.py:188
  43.6 1.9 %order.1 = f32[24,128]{1,0:T(8,128)} custom-call(f32[128,128]{1,0:T(8,128)} %bitcast.18), custom_call_target="tpu_custom_call" | custom-call | tf_op jit(solution)/shard_map/order/pallas_call | solution.py:189
  (1 shorter events, 0.0 us)
Async XLA Ops:
  2.2 4.5 %collective-permute-start.1 = (bf16[2,24,128]{2,1,0:T(8,128)(2,1)S(1)}, bf16[2,24,128]{2,1,0:T(8,128)(2,1)S(1)}, u32[]{:S(2)}, u32[]{:S(2)}) collective-permute-start(bf16[2,24,128]{2,1,0:T(8,128)(2,1)S(1)} %get-tuple-element.10), channel_id=1, source_target_pairs={{1,0},{2,1},{3,2},{0,3},{5,4},{6,5},{7,6},{4,7},{9,8},{10,9},{11,1... | collective-permute-start | bytes 36872 | tf_op jit(solution)/shard_map/ppermute | solution.py:166
  5.8 3.8 %collective-permute-start = (bf16[2,24,128]{2,1,0:T(8,128)(2,1)S(1)}, bf16[2,24,128]{2,1,0:T(8,128)(2,1)S(1)}, u32[]{:S(2)}, u32[]{:S(2)}) collective-permute-start(bf16[2,24,128]{2,1,0:T(8,128)(2,1)S(1)} %get-tuple-element.11), channel_id=1, source_target_pairs={{0,1},{1,2},{2,3},{3,0},{4,5},{5,6},{6,7},{7,4},{8,9},{9,10},{10,1... | collective-permute-start | bytes 36872 | tf_op jit(solution)/shard_map/ppermute | solution.py:165
  6.6 2.9 %copy-start = (bf16[2,24,128]{2,1,0:T(8,128)(2,1)}, bf16[2,24,128]{2,1,0:T(8,128)(2,1)S(1)}, u32[]{:S(2)}) copy-start(bf16[2,24,128]{2,1,0:T(8,128)(2,1)S(1)} %collective-permute-done.1.after) | copy-start | bytes 36868
  9.6 0.6 %copy-start.1 = (bf16[2,24,128]{2,1,0:T(8,128)(2,1)}, bf16[2,24,128]{2,1,0:T(8,128)(2,1)S(1)}, u32[]{:S(2)}) copy-start(bf16[2,24,128]{2,1,0:T(8,128)(2,1)S(1)} %collective-permute-done.before) | copy-start | bytes 36868

commit v2 on v1

--- a/solution.py
+++ b/solution.py
@@ -14,8 +14,9 @@
 TRACERS = 24
 LEVELS = 128
 COLS = 128
-GROUP = 4
+GROUP = 8
 SLOT = 32
+ROOM = 24 << 20
 
 F32 = jnp.float32
 BF16 = jnp.bfloat16
@@ -39,6 +40,19 @@
     above = jnp.concatenate([z[:1], z[:-1]], axis=0)
     below = jnp.concatenate([z[1:], z[-1:]], axis=0)
     return above + below - 2.0 * z
+
+
+def edge_kernel(fields, left, right, rows):
+    place = iota((8, COLS), 0)
+    lane = iota((8, COLS), 1)
+    edge = jnp.where(place < REACH, place, place + (COLS - 2 * REACH))
+    pick = (lane == edge).astype(BF16)
+    for q in range(TRACERS):
+        got = lax.dot_general(pick, fields[q], NT, preferred_element_type=F32)
+        for j in range(2 * REACH):
+            rows[j * TRACERS + q : j * TRACERS + q + 1, :] = got[j : j + 1]
+    left[...] = rows[: REACH * TRACERS].astype(BF16)
+    right[...] = rows[REACH * TRACERS :].astype(BF16)
 
 
 def main_kernel(
@@ -66,43 +80,37 @@
     far[...] = edge
     owner = place - (place // TRACERS) * TRACERS
     rows = jnp.concatenate(
-        [before[0], before[1], after[0], after[1], jnp.zeros((SLOT, LEVELS), BF16)], axis=0
+        [before[...], after[...], jnp.zeros((SLOT, LEVELS), BF16)], axis=0
     )
     halo[...] = rows.astype(F32).T.astype(BF16)
 
     count = cost[...]
     scale = coef[...].astype(F32) * (count.astype(F32) / (4.0 * KMAX))
     scale2 = jnp.concatenate([scale, scale], axis=1)
-    count2 = jnp.concatenate([count, count], axis=1)
+    count2 = jnp.concatenate([count, count], axis=1).astype(F32).astype(BF16)
     burden[...] = jnp.zeros((SLOT, COLS), F32)
 
-    def dynamics(q, carry):
+    for q in range(TRACERS):
         mine = jnp.where(owner == q, far[...], 0.0).astype(BF16)
         both = jnp.concatenate([fields[q], halo[...]], axis=1)
         summed = dot(both, jnp.concatenate([near[...], mine], axis=0))
         dyn[q] = (MIX * summed).astype(BF16)
-        return carry
-
-    lax.fori_loop(0, TRACERS, dynamics, 0, unroll=4)
 
     pairs = GROUP // 2
 
     def group(g, carry):
         base = g * GROUP
-        first = [
+        state = [
             jnp.concatenate([dyn[base + 2 * p], dyn[base + 2 * p + 1]], axis=1) for p in range(pairs)
         ]
-        state = list(first)
-        final = [None] * pairs
         for s in range(KMAX):
             for p in range(pairs):
                 both = dot(ops[s], state[p])
-                widened = both[:LEVELS] + scale2 * both[LEVELS:]
-                final[p] = widened if s == 0 else jnp.where(count2 > s, widened, final[p])
-                state[p] = widened.astype(BF16)
+                widened = (both[:LEVELS] + scale2 * both[LEVELS:]).astype(BF16)
+                state[p] = widened if s == 0 else jnp.where(count2 > s, widened, state[p])
         for p in range(pairs):
-            start = first[p].astype(F32)
-            change = final[p] - start
+            start = jnp.concatenate([dyn[base + 2 * p], dyn[base + 2 * p + 1]], axis=1).astype(F32)
+            change = state[p].astype(F32) - start
             total = jnp.sum(change, axis=0, keepdims=True)
             result = (start + change.astype(BF16).astype(F32)).astype(BF16)
             for i in range(2):
@@ -162,8 +170,18 @@
     up = [(i, (i + 1) % size) for i in range(size)]
     down = [(j, i) for i, j in up]
     flat = fields.reshape(TRACERS, LEVELS, COLS)
-    before = lax.ppermute(flat[:, :, COLS - REACH :].transpose(2, 0, 1), "narrow", up)
-    after = lax.ppermute(flat[:, :, :REACH].transpose(2, 0, 1), "narrow", down)
+    side = jax.ShapeDtypeStruct((REACH * TRACERS, LEVELS), BF16)
+    left, right = pl.pallas_call(
+        edge_kernel,
+        out_shape=(side, side),
+        in_specs=[pl.BlockSpec(memory_space=pltpu.VMEM)],
+        out_specs=[pl.BlockSpec(memory_space=pltpu.VMEM)] * 2,
+        scratch_shapes=[pltpu.VMEM((2 * REACH * TRACERS, LEVELS), F32)],
+        compiler_params=pltpu.CompilerParams(vmem_limit_bytes=ROOM),
+        name="edge",
+    )(flat)
+    before = lax.ppermute(right, "narrow", up)
+    after = lax.ppermute(left, "narrow", down)
     new, sent = pl.pallas_call(
         main_kernel,
         out_shape=(
@@ -180,6 +198,7 @@
             pltpu.VMEM((TRACERS, LEVELS, COLS), BF16),
             pltpu.VMEM((SLOT, COLS), F32),
         ],
+        compiler_params=pltpu.CompilerParams(vmem_limit_bytes=ROOM),
         name="physics",
     )(
         flat, before, after, neighbors.reshape(NEIGH, COLS), cost, dest,
@@ -191,6 +210,7 @@
         out_shape=jax.ShapeDtypeStruct((TRACERS, COLS), F32),
         in_specs=[pl.BlockSpec(memory_space=pltpu.VMEM)],
         out_specs=pl.BlockSpec(memory_space=pltpu.VMEM),
+        compiler_params=pltpu.CompilerParams(vmem_limit_bytes=ROOM),
         name="order",
     )(received)
     return new.reshape(fields.shape), burden[None]

time: 45.7 us -> 37.4 us (0.82)
  Pallas kernels: 15.8 us -> 8.8 us
  waiting for transfers between devices: 3.75 us -> 1.02 us
  blocking collectives: 19.5 us -> 21.3 us
    pallas_call x1, Pallas kernels: 13.9 us -> 7.22 us  [local(): pl.pallas_call(main_kernel, out_shape=(jax.ShapeDtypeStruct((TRACERS, LEV...]
    ppermute x2, waiting for transfers between devices: 3.75 us -> 1.02 us  [the longest x1 0.99 us: local(): before = lax.ppermute(right, 'narrow', up)]
    all_to_all x1, blocking collectives: 19.5 us -> 21.3 us  [local(): lax.all_to_all(sent, ('wide', 'narrow'), split_axis=0, concat_axis=0, til...]
    pallas_call x1, Pallas kernels: 1.91 us -> 1.07 us  [local(): pl.pallas_call(order_kernel, out_shape=jax.ShapeDtypeStruct((TRACERS, COL...]
    pallas_call x0 -> x1, Pallas kernels: none -> 0.51 us  [local(): pl.pallas_call(edge_kernel, out_shape=(side, side), in_specs=[pl.BlockSpe...]
    unnamed x5 -> x12, local copies, waits for them, and re-layouts: 2.14 us -> 1.79 us
  transfers between devices with their start and end apart: 2 -> 2, of which waited for: 2 -> 1; matrix products, arithmetic and copies ran while one was open for 0% -> 0% of each run, Pallas kernels for 0% -> 0%
where the time goes in v2:
time: 37.4 us; the launch traced here: 37.2 us
  blocking collectives  21.3 us (57%)
  Pallas kernels  8.8 us (24%)
  starting transfers between devices  3.67 us (10%)
  local copies, waits for them, and re-layouts  1.79 us (5%)
  waiting for transfers between devices  1.02 us (3%)
  between operations  0.66 us (2%)
    all_to_all x1, blocking collectives, local(): lax.all_to_all(sent, ('wide', 'narrow'), split_axis=0, concat_axis=0, til...  21.3 us
    pallas_call x1, Pallas kernels, local(): pl.pallas_call(main_kernel, out_shape=(jax.ShapeDtypeStruct((TRACERS, LEV...  7.22 us
    ppermute x1, starting transfers between devices, local(): before = lax.ppermute(right, 'narrow', up)  2.15 us
    unnamed x12, local copies, waits for them, and re-layouts  1.79 us
    ppermute x1, starting transfers between devices, local(): after = lax.ppermute(left, 'narrow', down)  1.53 us
    pallas_call x1, Pallas kernels, local(): pl.pallas_call(order_kernel, out_shape=jax.ShapeDtypeStruct((TRACERS, COL...  1.07 us
    ppermute x1, waiting for transfers between devices, local(): before = lax.ppermute(right, 'narrow', up)  0.99 us
  transfers between devices with their start and end apart: 2, of which 1 were waited for; matrix products, arithmetic and copies ran while one was open for 0% of the time, Pallas kernels for 0%

profile of v2, /device:TPU:1, one launch (start us, length us, event | category | flops | bytes accessed | tf_op | source)
XLA Modules:
  0.0 37.2 jit_solution(13237332458680952992)
XLA Ops:
  0.6 0.0 copy-start
  0.6 1.1 %copy-done = bf16[24,128,1,128]{3,1,2,0:T(8,128)(2,1)S(1)} copy-done((bf16[24,128,1,128]{3,1,2,0:T(8,128)(2,1)S(1)}, bf16[24,128,1,128]{3,1,2,0:T(8,128)(2,1)}, u32[]{:S(2)}) %copy-start) | copy-done | bytes 786456
  1.8 0.0 copy-start.1
  1.8 0.0 copy-start.2
  1.8 0.5 %edge.1 = (bf16[48,128]{1,0:T(8,128)(2,1)S(1)}, bf16[48,128]{1,0:T(8,128)(2,1)S(1)}) custom-call(bf16[24,128,128]{2,1,0:T(8,128)(2,1)S(1)} %bitcast.11), custom_call_target="tpu_custom_call" | custom-call | tf_op jit(solution)/shard_map/edge/pallas_call | solution.py:174
  2.3 2.1 %collective-permute-start = (bf16[48,128]{1,0:T(8,128)(2,1)S(1)}, bf16[48,128]{1,0:T(8,128)(2,1)S(1)}, u32[]{:S(2)}, u32[]{:S(2)}) collective-permute-start(bf16[48,128]{1,0:T(8,128)(2,1)S(1)} %get-tuple-element.6), channel_id=1, source_target_pairs={{0,1},{1,2},{2,3},{3,0},{4,5},{5,6},{6,7},{7,4},{8,9},{9,10},{10,1... | collective-permute-start | bytes 36872 | tf_op jit(solution)/shard_map/ppermute | solution.py:183
  4.4 0.0 copy-start.3
  4.4 1.5 %collective-permute-start.1 = (bf16[48,128]{1,0:T(8,128)(2,1)S(1)}, bf16[48,128]{1,0:T(8,128)(2,1)S(1)}, u32[]{:S(2)}, u32[]{:S(2)}) collective-permute-start(bf16[48,128]{1,0:T(8,128)(2,1)S(1)} %get-tuple-element.7), channel_id=1, source_target_pairs={{1,0},{2,1},{3,2},{0,3},{5,4},{6,5},{7,6},{4,7},{9,8},{10,9},{11,1... | collective-permute-start | bytes 36872 | tf_op jit(solution)/shard_map/ppermute | solution.py:184
  6.0 1.0 %collective-permute-done.before = bf16[48,128]{1,0:T(8,128)(2,1)S(1)} collective-permute-done((bf16[48,128]{1,0:T(8,128)(2,1)S(1)}, bf16[48,128]{1,0:T(8,128)(2,1)S(1)}, u32[]{:S(2)}, u32[]{:S(2)}) %collective-permute-start) | collective-permute-done | bytes 12320 | tf_op jit(solution)/shard_map/ppermute | solution.py:183
  6.9 0.0 collective-permute-done.1.after
  7.0 0.0 copy-start.4
  7.0 0.0 copy-start.5
  7.0 0.0 copy-done.1
  7.0 0.0 copy-done.2
  7.0 0.0 copy-done.3
  7.0 0.6 %copy-done.4 = s32[1,128]{1,0:T(1,128)S(1)} copy-done((s32[1,128]{1,0:T(1,128)S(1)}, s32[1,128]{1,0:T(1,128)}, u32[]{:S(2)}) %copy-start.4) | copy-done | bytes 536
  7.6 0.0 copy-done.5
  7.6 7.2 %physics.1 = (bf16[24,128,128]{2,1,0:T(8,128)(2,1)}, f32[128,128]{1,0:T(8,128)S(1)}) custom-call(bf16[24,128,128]{2,1,0:T(8,128)(2,1)S(1)} %bitcast.12, bf16[48,128]{1,0:T(8,128)(2,1)S(1)} %collective-permute-done.before, bf16[48,128]{1,0:T(8,128)(2,1)S(1)} %collective-permute-done.1.after, s32[4,128]{1,0:T(4,128)S(1)} %bitcast.16, s32[1,128]{1,0:T(1,128)S(1)} %copy-done.4, ...), custom_call_target="tpu_custom_call" | custom-call | tf_op jit(solution)/shard_map/physics/pallas_call | solution.py:185
  14.9 21.3 %all_to_all.11 = f32[128,1,128]{2,1,0:T(1,128)S(1)} all-to-all(f32[128,1,128]{2,1,0:T(1,128)S(1)} %bitcast.14), channel_id=1, replica_groups=mesh['wide'=32,'narrow'=4] {'wide','narrow'}, dimensions={0} | all-to-all | bytes 131072 | tf_op jit(solution)/shard_map/all_to_all | solution.py:207
  36.1 1.1 %order.1 = f32[24,128]{1,0:T(8,128)} custom-call(f32[128,128]{1,0:T(8,128)S(1)} %bitcast.13), custom_call_target="tpu_custom_call" | custom-call | tf_op jit(solution)/shard_map/order/pallas_call | solution.py:208
Async XLA Ops:
  0.6 1.1 %copy-start = (bf16[24,128,1,128]{3,1,2,0:T(8,128)(2,1)S(1)}, bf16[24,128,1,128]{3,1,2,0:T(8,128)(2,1)}, u32[]{:S(2)}) copy-start(bf16[24,128,1,128]{3,1,2,0:T(8,128)(2,1)} %param.6) | copy-start | bytes 2359300
  1.8 5.2 %copy-start.1 = (bf16[8,128,128]{2,1,0:T(8,128)(2,1)S(1)}, bf16[8,128,128]{2,1,0:T(8,128)(2,1)}, u32[]{:S(2)}) copy-start(bf16[8,128,128]{2,1,0:T(8,128)(2,1)} %operators.1) | copy-start | bytes 786436
  1.8 5.2 %copy-start.2 = (bf16[128,1,128]{2,0,1:T(8,128)(2,1)S(1)}, bf16[128,1,128]{2,0,1:T(8,128)(2,1)}, u32[]{:S(2)}) copy-start(bf16[128,1,128]{2,0,1:T(8,128)(2,1)} %param.10) | copy-start | bytes 98308
  2.3 4.7 %collective-permute-start = (bf16[48,128]{1,0:T(8,128)(2,1)S(1)}, bf16[48,128]{1,0:T(8,128)(2,1)S(1)}, u32[]{:S(2)}, u32[]{:S(2)}) collective-permute-start(bf16[48,128]{1,0:T(8,128)(2,1)S(1)} %get-tuple-element.6), channel_id=1, source_target_pairs={{0,1},{1,2},{2,3},{3,0},{4,5},{5,6},{6,7},{7,4},{8,9},{9,10},{10,1... | collective-permute-start | bytes 36872 | tf_op jit(solution)/shard_map/ppermute | solution.py:183
  4.4 2.6 %copy-start.3 = (s32[4,1,128]{2,1,0:T(1,128)S(1)}, s32[4,1,128]{2,1,0:T(1,128)}, u32[]{:S(2)}) copy-start(s32[4,1,128]{2,1,0:T(1,128)} %param.7) | copy-start | bytes 6148
  4.4 2.5 %collective-permute-start.1 = (bf16[48,128]{1,0:T(8,128)(2,1)S(1)}, bf16[48,128]{1,0:T(8,128)(2,1)S(1)}, u32[]{:S(2)}, u32[]{:S(2)}) collective-permute-start(bf16[48,128]{1,0:T(8,128)(2,1)S(1)} %get-tuple-element.7), channel_id=1, source_target_pairs={{1,0},{2,1},{3,2},{0,3},{5,4},{6,5},{7,6},{4,7},{9,8},{10,9},{11,1... | collective-permute-start | bytes 36872 | tf_op jit(solution)/shard_map/ppermute | solution.py:184
  7.0 0.7 %copy-start.4 = (s32[1,128]{1,0:T(1,128)S(1)}, s32[1,128]{1,0:T(1,128)}, u32[]{:S(2)}) copy-start(s32[1,128]{1,0:T(1,128)} %cost.1) | copy-start | bytes 1540
  7.0 0.7 %copy-start.5 = (s32[1,128]{1,0:T(1,128)S(1)}, s32[1,128]{1,0:T(1,128)}, u32[]{:S(2)}) copy-start(s32[1,128]{1,0:T(1,128)} %dest.1) | copy-start | bytes 1540

commit v3 on v2

v3 whole, which is shorter than its diff:
```python
import functools

import jax
import jax.numpy as jnp
from jax import lax
from jax.experimental import pallas as pl
from jax.experimental.pallas import tpu as pltpu
from jax.sharding import PartitionSpec as P

REACH = 2
NEIGH = 4
KMAX = 8
MIX = 0.2
TRACERS = 24
LEVELS = 128
COLS = 128
GROUP = 12
SLOT = 32
TILE = 16
ROOM = 24 << 20

F32 = jnp.float32
BF16 = jnp.bfloat16
NT = (((1,), (1,)), ((), ()))


def iota(shape, dim):
    return lax.broadcasted_iota(jnp.int32, shape, dim)


def dot(a, b):
    return jnp.dot(a, b, preferred_element_type=F32)


def split(x):
    high = x.astype(BF16)
    return high, (x - high.astype(F32)).astype(BF16)


def level_laplace(z):
    above = jnp.concatenate([z[:1], z[:-1]], axis=0)
    below = jnp.concatenate([z[1:], z[-1:]], axis=0)
    return above + below - 2.0 * z


def edge_kernel(fields, left, right, rows):
    place = iota((8, COLS), 0)
    lane = iota((8, COLS), 1)
    edge = jnp.where(place < REACH, place, place + (COLS - 2 * REACH))
    pick = (lane == edge).astype(BF16)
    for q in range(TRACERS):
        got = lax.dot_general(pick, fields[q], NT, preferred_element_type=F32)
        for j in range(2 * REACH):
            rows[j * TRACERS + q : j * TRACERS + q + 1, :] = got[j : j + 1]
    left[...] = rows[: REACH * TRACERS].astype(BF16)
    right[...] = rows[REACH * TRACERS :].astype(BF16)


def plan_kernel(
    neighbors, cost, dest, coef, operators, ops, near, far, scale, pull, picked, pair
):
    for s in range(KMAX):
        op = operators[s]
        lap = level_laplace(op.astype(F32)).astype(BF16)
        pair[s, :LEVELS] = op
        pair[s, LEVELS:] = lap
        for t in range(LEVELS // TILE):
            ops[s, 2 * t * TILE : (2 * t + 1) * TILE] = op[t * TILE : (t + 1) * TILE]
            ops[s, (2 * t + 1) * TILE : (2 * t + 2) * TILE] = lap[t * TILE : (t + 1) * TILE]

    place = iota((COLS, COLS), 0)
    here = iota((COLS, COLS), 1)
    lane = iota((1, COLS), 1)
    weight = (place == here).astype(F32)
    edge = jnp.zeros((COLS, COLS), F32)
    tag = place // TRACERS
    tag = jnp.where(tag < REACH, tag - REACH, tag + (COLS - REACH))
    for k in range(NEIGH):
        offset = ((neighbors[k : k + 1, :] - lane + REACH) & (COLS - 1)) - REACH
        reads = lane + offset
        weight += (place == reads).astype(F32)
        edge += (tag == reads).astype(F32)
    near[...] = weight.astype(BF16)
    far[...] = edge
    steps = jnp.broadcast_to(cost[...].astype(F32), (COLS, COLS))
    scaled = coef[...].astype(F32) * (steps / (4.0 * KMAX))
    scale[...] = scaled

    scaled = scaled.T
    steps = steps.T
    row = jnp.ones((COLS, LEVELS), F32)
    for s in reversed(range(KMAX)):
        parts = []
        for part in zip(split(row), split(scaled * row)):
            parts.append(jnp.concatenate(part, axis=1))
        moved = dot(jnp.concatenate(parts, axis=0), pair[s])
        row = jnp.where(steps > s, moved[:COLS] + moved[COLS:], 1.0)
    pull[...] = (row - 1.0).T

    target = jnp.broadcast_to(dest[...], (COLS, COLS)).astype(F32)
    same = (target.T == target) & (place < here)
    turn = jnp.sum(same.astype(F32), axis=0, keepdims=True)
    to = (target == place.astype(F32)).astype(F32)
    picked[:, :COLS] = (to * (turn == 0.0)).astype(BF16)
    picked[:, COLS:] = (to * (turn == 1.0)).astype(BF16)


def start_kernel(fields, before, after, near, far, pull, picked, dyn, sent, halo, burden):
    rows = jnp.concatenate(
        [before[...], after[...], jnp.zeros((SLOT, LEVELS), BF16)], axis=0
    )
    halo[...] = rows.astype(F32).T.astype(BF16)
    place = iota((COLS, COLS), 0)
    owner = place - (place // TRACERS) * TRACERS
    burden[TRACERS:] = (iota((SLOT - TRACERS, COLS), 0) == 0).astype(F32)

    for q in range(TRACERS):
        mine = jnp.where(owner == q, far[...], 0.0).astype(BF16)
        both = jnp.concatenate([fields[q], halo[...]], axis=1)
        summed = dot(both, jnp.concatenate([near[...], mine], axis=0))
        start = (MIX * summed).astype(BF16)
        dyn[q] = start
        burden[q : q + 1, :] = jnp.sum(pull[...] * start.astype(F32), axis=0, keepdims=True)

    none = jnp.zeros((SLOT, COLS), BF16)
    total = jnp.zeros((COLS, COLS), F32)
    for part in split(burden[...]):
        wide = jnp.concatenate(
            [
                jnp.concatenate([part, none], axis=1),
                jnp.concatenate([none, part], axis=1),
                jnp.zeros((2 * SLOT, 2 * COLS), BF16),
            ],
            axis=0,
        )
        total += lax.dot_general(picked[...], wide, NT, preferred_element_type=F32)
    sent[...] = total


def main_kernel(dyn, ops, scale, cost, out):
    count = cost[...].astype(F32).astype(BF16)
    count2 = jnp.concatenate([count, count], axis=1)
    pairs = GROUP // 2

    def begin(base, p):
        return jnp.concatenate([dyn[base + 2 * p], dyn[base + 2 * p + 1]], axis=1)

    def group(g, carry):
        base = g * GROUP
        state = [begin(base, p) for p in range(pairs)]
        for s in range(KMAX):
            for p in range(pairs):
                both = dot(ops[s], state[p])
                tiles = []
                for t in range(LEVELS // TILE):
                    flat = both[2 * t * TILE : (2 * t + 1) * TILE]
                    bent = both[(2 * t + 1) * TILE : (2 * t + 2) * TILE]
                    factor = scale[t * TILE : (t + 1) * TILE]
                    factor = jnp.concatenate([factor, factor], axis=1)
                    tiles.append((flat + factor * bent).astype(BF16))
                widened = jnp.concatenate(tiles, axis=0)
                state[p] = widened if s == 0 else jnp.where(count2 > s, widened, state[p])
        for p in range(pairs):
            start = begin(base, p)
            result = start + (state[p] - start)
            for i in range(2):
                out[base + 2 * p + i] = result[:, i * COLS : (i + 1) * COLS]
        return carry

    lax.fori_loop(0, TRACERS // GROUP, group, 0)


def order_kernel(received, out):
    values = received[...]
    place = iota((COLS, COLS), 0)
    here = iota((COLS, COLS), 1)
    flags = values.astype(BF16)
    earlier = dot((here < place).astype(BF16), flags)
    first = values[:, TRACERS : TRACERS + 1]
    second = values[:, SLOT + TRACERS : SLOT + TRACERS + 1]
    rank = earlier[:, TRACERS : TRACERS + 1] + earlier[:, SLOT + TRACERS : SLOT + TRACERS + 1]
    spot = here.astype(F32)
    chosen = jnp.concatenate(
        [
            jnp.where(spot == rank, first, 0.0),
            jnp.where(spot == rank + first, second, 0.0),
        ],
        axis=0,
    ).astype(BF16)
    turned = values.T
    rows = jnp.concatenate([turned[:SLOT], turned[SLOT : 2 * SLOT]], axis=1)
    high, low = split(rows)
    out[...] = (dot(high, chosen) + dot(low, chosen))[:TRACERS]


def local(fields, neighbors, cost, dest, diffusivity, operators):
    size = lax.axis_size("narrow")
    up = [(i, (i + 1) % size) for i in range(size)]
    down = [(j, i) for i, j in up]
    flat = fields.reshape(TRACERS, LEVELS, COLS)
    vmem = pl.BlockSpec(memory_space=pltpu.VMEM)
    params = pltpu.CompilerParams(vmem_limit_bytes=ROOM)
    side = jax.ShapeDtypeStruct((REACH * TRACERS, LEVELS), BF16)
    left, right = pl.pallas_call(
        edge_kernel,
        out_shape=(side, side),
        in_specs=[vmem],
        out_specs=[vmem] * 2,
        scratch_shapes=[pltpu.VMEM((2 * REACH * TRACERS, LEVELS), F32)],
        compiler_params=params,
        name="edge",
    )(flat)
    before = lax.ppermute(right, "narrow", up)
    after = lax.ppermute(left, "narrow", down)
    square = jax.ShapeDtypeStruct((COLS, COLS), F32)
    ops, near, far, scale, pull, picked = pl.pallas_call(
        plan_kernel,
        out_shape=(
            jax.ShapeDtypeStruct((KMAX, 2 * LEVELS, LEVELS), BF16),
            jax.ShapeDtypeStruct((COLS, COLS), BF16),
            square,
            square,
            square,
            jax.ShapeDtypeStruct((COLS, 2 * COLS), BF16),
        ),
        in_specs=[vmem] * 5,
        out_specs=[vmem] * 6,
        scratch_shapes=[pltpu.VMEM((KMAX, 2 * LEVELS, LEVELS), BF16)],
        compiler_params=params,
        cost_estimate=pl.CostEstimate(flops=10**7, bytes_accessed=10**6, transcendentals=0),
        name="plan",
    )(
        *[
            pltpu.with_memory_space_constraint(x, pltpu.HBM)
            for x in (
                neighbors.reshape(NEIGH, COLS), cost, dest,
                diffusivity.reshape(LEVELS, COLS), operators,
            )
        ]
    )
    dyn, sent = pl.pallas_call(
        start_kernel,
        out_shape=(jax.ShapeDtypeStruct(flat.shape, BF16), square),
        in_specs=[vmem] * 7,
        out_specs=[vmem] * 2,
        scratch_shapes=[pltpu.VMEM((LEVELS, COLS), BF16), pltpu.VMEM((SLOT, COLS), F32)],
        compiler_params=params,
        name="start",
    )(flat, before, after, near, far, pull, picked)
    received = lax.all_to_all(sent, ("wide", "narrow"), split_axis=0, concat_axis=0, tiled=True)
    new = pl.pallas_call(
        main_kernel,
        out_shape=jax.ShapeDtypeStruct(flat.shape, BF16),
        in_specs=[vmem] * 4,
        out_specs=vmem,
        compiler_params=params,
        cost_estimate=pl.CostEstimate(flops=10**10, bytes_accessed=10**7, transcendentals=0),
        name="physics",
    )(dyn, ops, scale, cost)
    burden = pl.pallas_call(
        order_kernel,
        out_shape=jax.ShapeDtypeStruct((TRACERS, COLS), F32),
        in_specs=[vmem],
        out_specs=vmem,
        compiler_params=params,
        name="order",
    )(received)
    return new.reshape(fields.shape), burden[None]


def solution(mesh):
    in_specs = (
        P(None, None, "wide", "narrow"),
        P(None, "wide", "narrow"),
        P("wide", "narrow"),
        P("wide", "narrow"),
        P(None, "wide", "narrow"),
        P(),
    )
    out_specs = (P(None, None, "wide", "narrow"), P(("wide", "narrow"), None, None))
    return jax.shard_map(local, mesh=mesh, in_specs=in_specs, out_specs=out_specs, check_vma=False)
```

time: 37.4 us -> 31.2 us (0.83)
  blocking collectives: 21.3 us -> 0 us
  starting transfers between devices: 3.67 us -> 14 us
  waiting for transfers between devices: 1.02 us -> 4.53 us
  Pallas kernels: 8.8 us -> 10.1 us
    all_to_all x1 -> x0, blocking collectives: 21.3 us -> none  [local(): lax.all_to_all(sent, ('wide', 'narrow'), split_axis=0, concat_axis=0, til...]
    all_to_all x0 -> x1, starting transfers between devices: none -> 10.3 us  [local(): lax.all_to_all(sent, ('wide', 'narrow'), split_axis=0, concat_axis=0, til...]
    all_to_all x0 -> x1, waiting for transfers between devices: none -> 4.52 us  [local(): lax.all_to_all(sent, ('wide', 'narrow'), split_axis=0, concat_axis=0, til...]
    pallas_call x2 -> x4, Pallas kernels: 7.73 us -> 8.99 us  [the longest x1 4.49 us: local(): pl.pallas_call(main_kernel, out_shape=jax.ShapeDtypeStruct(flat.shape, BF...]
    ppermute x1, waiting for transfers between devices: 0.99 us -> 0.01 us  [local(): before = lax.ppermute(right, 'narrow', up)]
    unnamed x12 -> x6, local copies, waits for them, and re-layouts: 1.79 us -> 1.78 us
  transfers between devices with their start and end apart: 2 -> 3, of which waited for: 1 -> 1; matrix products, arithmetic and copies ran while one was open for 0% -> 0% of each run, Pallas kernels for 0% -> 22%
where the time goes in v3:
time: 31.2 us; the launch traced here: 31 us
  starting transfers between devices  14 us (45%)
  Pallas kernels  10.1 us (32%)
  waiting for transfers between devices  4.53 us (15%)
  local copies, waits for them, and re-layouts  1.78 us (6%)
  between operations  0.68 us (2%)
    all_to_all x1, starting transfers between devices, local(): lax.all_to_all(sent, ('wide', 'narrow'), split_axis=0, concat_axis=0, til...  10.3 us
    all_to_all x1, waiting for transfers between devices, local(): lax.all_to_all(sent, ('wide', 'narrow'), split_axis=0, concat_axis=0, til...  4.52 us
    pallas_call x1, Pallas kernels, local(): pl.pallas_call(main_kernel, out_shape=jax.ShapeDtypeStruct(flat.shape, BF...  4.49 us
    pallas_call x1, Pallas kernels, local(): pl.pallas_call(plan_kernel, out_shape=(jax.ShapeDtypeStruct((KMAX, 2 * LE...  2.48 us
    ppermute x1, starting transfers between devices, local(): before = lax.ppermute(right, 'narrow', up)  2.15 us
    unnamed x6, local copies, waits for them, and re-layouts  1.78 us
    ppermute x1, starting transfers between devices, local(): after = lax.ppermute(left, 'narrow', down)  1.52 us
    pallas_call x1, Pallas kernels, local(): pl.pallas_call(start_kernel, out_shape=(jax.ShapeDtypeStruct(flat.shape,...  1.51 us
  transfers between devices with their start and end apart: 3, of which 1 were waited for; matrix products, arithmetic and copies ran while one was open for 0% of the time, Pallas kernels for 22%

profile of v3, /device:TPU:1, one launch (start us, length us, event | category | flops | bytes accessed | tf_op | source)
XLA Modules:
  0.0 31.0 jit_solution(15547438437904499570)
XLA Ops:
  0.6 0.0 copy-start
  0.6 1.1 %copy-done = bf16[24,128,1,128]{3,1,2,0:T(8,128)(2,1)S(1)} copy-done((bf16[24,128,1,128]{3,1,2,0:T(8,128)(2,1)S(1)}, bf16[24,128,1,128]{3,1,2,0:T(8,128)(2,1)}, u32[]{:S(2)}) %copy-start) | copy-done | bytes 786456
  1.8 0.0 copy-start.1
  1.8 0.5 %edge.1 = (bf16[48,128]{1,0:T(8,128)(2,1)S(1)}, bf16[48,128]{1,0:T(8,128)(2,1)S(1)}) custom-call(bf16[24,128,128]{2,1,0:T(8,128)(2,1)S(1)} %bitcast.11), custom_call_target="tpu_custom_call" | custom-call | tf_op jit(solution)/shard_map/edge/pallas_call | solution.py:204
  2.3 2.1 %collective-permute-start = (bf16[48,128]{1,0:T(8,128)(2,1)S(1)}, bf16[48,128]{1,0:T(8,128)(2,1)S(1)}, u32[]{:S(2)}, u32[]{:S(2)}) collective-permute-start(bf16[48,128]{1,0:T(8,128)(2,1)S(1)} %get-tuple-element.12), channel_id=1, source_target_pairs={{0,1},{1,2},{2,3},{3,0},{4,5},{5,6},{6,7},{7,4},{8,9},{9,10},{10,1... | collective-permute-start | bytes 36872 | tf_op jit(solution)/shard_map/ppermute | solution.py:213
  4.4 1.5 %collective-permute-start.1 = (bf16[48,128]{1,0:T(8,128)(2,1)S(1)}, bf16[48,128]{1,0:T(8,128)(2,1)S(1)}, u32[]{:S(2)}, u32[]{:S(2)}) collective-permute-start(bf16[48,128]{1,0:T(8,128)(2,1)S(1)} %get-tuple-element.13), channel_id=1, source_target_pairs={{1,0},{2,1},{3,2},{0,3},{5,4},{6,5},{7,6},{4,7},{9,8},{10,9},{11,1... | collective-permute-start | bytes 36872 | tf_op jit(solution)/shard_map/ppermute | solution.py:214
  5.9 2.5 %plan.1 = (bf16[8,256,128]{2,1,0:T(8,128)(2,1)S(1)}, bf16[128,128]{1,0:T(8,128)(2,1)S(1)}, f32[128,128]{1,0:T(8,128)S(1)}, f32[128,128]{1,0:T(8,128)S(1)}, f32[1...) custom-call(s32[4,128]{1,0:T(4,128)} %bitcast.16, s32[1,128]{1,0:T(1,128)} %cost.3, s32[1,128]{1,0:T(1,128)} %dest.1, ...), custom_call_target="tpu_custom_call" | custom-call | flops 10000000 | bytes 1000000 | tf_op jit(solution)/shard_map/plan/pallas_call | solution.py:216
  8.4 0.0 collective-permute-done.before
  8.4 0.0 collective-permute-done.1.after
  8.4 0.0 copy-done.1
  8.5 1.5 %start.1 = (bf16[24,128,128]{2,1,0:T(8,128)(2,1)S(1)}, f32[128,128]{1,0:T(8,128)}) custom-call(bf16[24,128,128]{2,1,0:T(8,128)(2,1)S(1)} %bitcast.12, bf16[48,128]{1,0:T(8,128)(2,1)S(1)} %collective-permute-done.before, bf16[48,128]{1,0:T(8,128)(2,1)S(1)} %collective-permute-done.1.after, bf16[128,128]{1,0:T(8,128)(2,1)S(1)} %get-tuple-element.14.near, ...), custom_call_target="tpu_custom_call" | custom-call | tf_op jit(solution)/shard_map/start/pallas_call | solution.py:241
  10.0 10.3 %all-to-all-start = ((f32[128,1,128]{2,1,0:T(1,128)}), f32[128,1,128]{2,1,0:T(1,128)S(1)}, u32[]{:S(2)}, u32[]{:S(2)}) async-start(f32[128,1,128]{2,1,0:T(1,128)} %bitcast.6), calls=%async_computation | async-start | bytes 131072 | tf_op jit(solution)/shard_map/all_to_all | solution.py:250
  20.3 0.0 copy-start.2
  20.3 0.6 %copy-done.2 = s32[1,128]{1,0:T(1,128)S(1)} copy-done((s32[1,128]{1,0:T(1,128)S(1)}, s32[1,128]{1,0:T(1,128)}, u32[]{:S(2)}) %copy-start.2) | copy-done | bytes 536
  20.9 4.5 %physics.1 = bf16[24,128,128]{2,1,0:T(8,128)(2,1)} custom-call(bf16[24,128,128]{2,1,0:T(8,128)(2,1)S(1)} %get-tuple-element.18.dyn, bf16[8,256,128]{2,1,0:T(8,128)(2,1)S(1)} %get-tuple-element.19.ops, f32[128,128]{1,0:T(8,128)S(1)} %get-tuple-element.20.scale, s32[1,128]{1,0:T(1,128)S(1)} %copy-done.2), custom_call_target="tpu_custom_call" | custom-call | flops 10000000000 | bytes 10000000 | tf_op jit(solution)/shard_map/physics/pallas_call | solution.py:251
  25.4 4.5 %all-to-all-done = f32[128,1,128]{2,1,0:T(1,128)S(1)} async-done(((f32[128,1,128]{2,1,0:T(1,128)}), f32[128,1,128]{2,1,0:T(1,128)S(1)}, u32[]{:S(2)}, u32[]{:S(2)}) %all-to-all-start) | async-done | bytes 65568 | tf_op jit(solution)/shard_map/all_to_all | solution.py:250
  29.9 1.1 %order.1 = f32[24,128]{1,0:T(8,128)} custom-call(f32[128,128]{1,0:T(8,128)S(1)} %bitcast.13), custom_call_target="tpu_custom_call" | custom-call | tf_op jit(solution)/shard_map/order/pallas_call | solution.py:260
Async XLA Ops:
  0.6 1.1 %copy-start = (bf16[24,128,1,128]{3,1,2,0:T(8,128)(2,1)S(1)}, bf16[24,128,1,128]{3,1,2,0:T(8,128)(2,1)}, u32[]{:S(2)}) copy-start(bf16[24,128,1,128]{3,1,2,0:T(8,128)(2,1)} %param.6) | copy-start | bytes 2359300
  1.8 6.7 %copy-start.1 = (bf16[24,128,1,128]{3,1,2,0:T(8,128)(2,1)S(1)}, bf16[24,128,1,128]{3,1,2,0:T(8,128)(2,1)}, u32[]{:S(2)}) copy-start(bf16[24,128,1,128]{3,1,2,0:T(8,128)(2,1)} %param.6) | copy-start | bytes 2359300
  2.3 6.2 %collective-permute-start = (bf16[48,128]{1,0:T(8,128)(2,1)S(1)}, bf16[48,128]{1,0:T(8,128)(2,1)S(1)}, u32[]{:S(2)}, u32[]{:S(2)}) collective-permute-start(bf16[48,128]{1,0:T(8,128)(2,1)S(1)} %get-tuple-element.12), channel_id=1, source_target_pairs={{0,1},{1,2},{2,3},{3,0},{4,5},{5,6},{6,7},{7,4},{8,9},{9,10},{10,1... | collective-permute-start | bytes 36872 | tf_op jit(solution)/shard_map/ppermute | solution.py:213
  4.4 4.0 %collective-permute-start.1 = (bf16[48,128]{1,0:T(8,128)(2,1)S(1)}, bf16[48,128]{1,0:T(8,128)(2,1)S(1)}, u32[]{:S(2)}, u32[]{:S(2)}) collective-permute-start(bf16[48,128]{1,0:T(8,128)(2,1)S(1)} %get-tuple-element.13), channel_id=1, source_target_pairs={{1,0},{2,1},{3,2},{0,3},{5,4},{6,5},{7,6},{4,7},{9,8},{10,9},{11,1... | collective-permute-start | bytes 36872 | tf_op jit(solution)/shard_map/ppermute | solution.py:214
  10.0 20.0 %all-to-all-start = ((f32[128,1,128]{2,1,0:T(1,128)}), f32[128,1,128]{2,1,0:T(1,128)S(1)}, u32[]{:S(2)}, u32[]{:S(2)}) async-start(f32[128,1,128]{2,1,0:T(1,128)} %bitcast.6), calls=%async_computation | async-start | bytes 131072 | tf_op jit(solution)/shard_map/all_to_all | solution.py:250
  20.3 0.7 %copy-start.2 = (s32[1,128]{1,0:T(1,128)S(1)}, s32[1,128]{1,0:T(1,128)}, u32[]{:S(2)}) copy-start(s32[1,128]{1,0:T(1,128)} %cost.3) | copy-start | bytes 1540

commit v4 on v3

v4 whole, which is shorter than its diff:
```python
import functools

import jax
import jax.numpy as jnp
from jax import lax
from jax.experimental import pallas as pl
from jax.experimental.pallas import tpu as pltpu
from jax.sharding import PartitionSpec as P

REACH = 2
NEIGH = 4
KMAX = 8
MIX = 0.2
TRACERS = 24
LEVELS = 128
COLS = 128
GROUP = 12
SLOT = 32
TILE = 16
TURNS = TILE // REACH
SIDE = REACH * TRACERS
NEAR = 8
CHAINS = 2
ROOM = 24 << 20

F32 = jnp.float32
BF16 = jnp.bfloat16
NT = (((1,), (1,)), ((), ()))


def iota(shape, dim):
    return lax.broadcasted_iota(jnp.int32, shape, dim)


def dot(a, b):
    return jnp.dot(a, b, preferred_element_type=F32)


def split(x):
    high = x.astype(BF16)
    return high, (x - high.astype(F32)).astype(BF16)


def level_laplace(z):
    above = jnp.concatenate([z[:1], z[:-1]], axis=0)
    below = jnp.concatenate([z[1:], z[-1:]], axis=0)
    return above + below - 2.0 * z


def edge_kernel(fields, left, right, own, left_rows, right_rows, own_rows):
    place = iota((NEAR, COLS), 0)
    lane = iota((NEAR, COLS), 1)
    edge = jnp.where(place < NEAR // 2, place, place + (COLS - NEAR))
    pick = (lane == edge).astype(BF16)
    for q in range(TRACERS):
        got = lax.dot_general(pick, fields[q], NT, preferred_element_type=F32)
        own_rows[NEAR * q : NEAR * (q + 1)] = got
        left_rows[REACH * q : REACH * (q + 1)] = got[:REACH]
        right_rows[REACH * q : REACH * (q + 1)] = got[NEAR - REACH :]
    left[...] = left_rows[...].astype(BF16)
    right[...] = right_rows[...].astype(BF16)
    own[: NEAR * TRACERS] = own_rows[...].astype(BF16)
    own[NEAR * TRACERS :] = jnp.zeros((2 * COLS - NEAR * TRACERS, LEVELS), BF16)


def halo_rows(before, after):
    gap = jnp.zeros((COLS // 2 - SIDE, LEVELS), BF16)
    return jnp.concatenate([before[...], gap, after[...], gap], axis=0)


def slots(values, axis):
    none = jnp.zeros(values.shape, values.dtype)
    first = jnp.concatenate([values, none], axis=axis)
    second = jnp.concatenate([none, values], axis=axis)
    return first, second


def plan_kernel(
    fields, own, meta, coef, operators,
    ops, near, far, scale, picked_edge, reach_edge, pull_edge, base_edge, count, base,
    pair, start, burden,
):
    for s in reversed(range(KMAX)):
        op = operators[s]
        lap = level_laplace(op.astype(F32)).astype(BF16)
        pair[s, :LEVELS] = op
        pair[s, LEVELS:] = lap
        for t in range(LEVELS // TILE):
            ops[s, 2 * t * TILE : (2 * t + 1) * TILE] = op[t * TILE : (t + 1) * TILE]
            ops[s, (2 * t + 1) * TILE : (2 * t + 2) * TILE] = lap[t * TILE : (t + 1) * TILE]

    steps = meta[NEIGH : NEIGH + 1, :].astype(F32)
    count[...] = steps
    steps = jnp.broadcast_to(steps, (COLS, COLS))
    scaled = coef[...].astype(F32) * (steps / (4.0 * KMAX))
    scale[...] = scaled
    scaled = scaled.T
    steps = steps.T

    place = iota((COLS, COLS), 0)
    here = iota((COLS, COLS), 1)
    lane = iota((1, COLS), 1)
    half = COLS // 2
    outer = jnp.where(place < half, place % REACH - REACH, place % REACH + COLS)
    inner = jnp.where(place < half, place % REACH, place % REACH + (COLS - REACH))
    weight = (place == here).astype(F32)
    reach = jnp.zeros((COLS, COLS), F32)
    row16 = iota((TILE, COLS), 0)
    turn16 = row16 % REACH
    before = jnp.zeros((TILE, COLS), F32)
    after = jnp.zeros((TILE, COLS), F32)
    for k in range(NEIGH):
        offset = ((meta[k : k + 1, :] - lane + REACH) & (COLS - 1)) - REACH
        reads = lane + offset
        weight += (place == reads).astype(F32)
        reach += (outer == reads).astype(F32)
        before += (turn16 - REACH == reads).astype(F32)
        after += (turn16 + COLS == reads).astype(F32)
    near[...] = weight.astype(BF16)
    for v in range(TURNS):
        mine = row16 // REACH == v
        far[0, v] = jnp.where(mine, before, 0.0).astype(BF16)
        far[1, v] = jnp.where(mine, after, 0.0).astype(BF16)

    target = jnp.broadcast_to(meta[NEIGH + 1 : NEIGH + 2, :], (COLS, COLS)).astype(F32)
    same = (target.T == target) & (place < here)
    turn = jnp.sum(same.astype(F32), axis=0, keepdims=True)
    to = (target == place.astype(F32)).astype(F32)
    picked = jnp.concatenate(
        [(to * (turn == 0.0)).astype(BF16), (to * (turn == 1.0)).astype(BF16)], axis=1
    )

    chosen = (inner == here).astype(BF16)
    for i in range(2):
        cols = slice(i * COLS, (i + 1) * COLS)
        picked_edge[:, cols] = lax.dot_general(
            picked[:, cols], chosen, NT, preferred_element_type=F32
        ).astype(BF16)
    tracer = (place % half) // REACH
    got = lax.dot_general(chosen, reach.astype(BF16), NT, preferred_element_type=F32)
    reach_edge[...] = jnp.where(tracer == (here % half) // REACH, got, 0.0).astype(BF16)
    got = lax.dot_general(chosen, near[...], NT, preferred_element_type=F32).astype(BF16)
    wide = (COLS, 2 * COLS)
    col = iota(wide, 1) % NEAR
    col = jnp.where(col < NEAR // 2, col, col + (COLS - NEAR))
    got = dot(got, (iota(wide, 0) == col).astype(BF16))
    mine = (iota(wide, 0) % half) // REACH == iota(wide, 1) // NEAR
    base_edge[...] = dot(jnp.where(mine, got, 0.0).astype(BF16), own[...])

    part = COLS // CHAINS
    held = [slice(i * part, (i + 1) * part) for i in range(CHAINS)]
    state = [jnp.ones((part, LEVELS), F32)] * CHAINS
    for s in reversed(range(KMAX)):
        for i, cols in enumerate(held):
            parts = []
            for pieces in zip(split(state[i]), split(scaled[cols] * state[i])):
                parts.append(jnp.concatenate(pieces, axis=1))
            moved = dot(jnp.concatenate(parts, axis=0), pair[s])
            state[i] = jnp.where(steps[cols] > s, moved[:part] + moved[part:], 1.0)
        for q in range((KMAX - 1 - s) * TRACERS // KMAX, (KMAX - s) * TRACERS // KMAX):
            start[q] = (MIX * dot(fields[q], near[...])).astype(BF16)
    pull = jnp.concatenate(state, axis=0) - 1.0
    high, low = split(pull)
    pull_edge[...] = dot(chosen, high) + dot(chosen, low)
    pull = pull.T

    for q in range(TRACERS):
        burden[q : q + 1, :] = jnp.sum(pull * start[q].astype(F32), axis=0, keepdims=True)
    inside = (lane >= REACH) & (lane < COLS - REACH)
    values = jnp.where(inside, burden[...], 0.0)
    flags = (iota((SLOT - TRACERS, COLS), 0) == 0).astype(F32)
    total = jnp.zeros((COLS, COLS), F32)
    for part in split(jnp.concatenate([values, flags], axis=0)):
        rows = [*slots(part, 1), jnp.zeros((2 * SLOT, 2 * COLS), BF16)]
        total += lax.dot_general(
            picked, jnp.concatenate(rows, axis=0), NT, preferred_element_type=F32
        )
    base[...] = total


def start_kernel(before, after, picked_edge, reach_edge, pull_edge, base_edge, base, sent):
    summed = base_edge[...] + dot(reach_edge[...], halo_rows(before, after))
    start = (MIX * summed).astype(BF16).astype(F32)
    values = jnp.sum(pull_edge[...] * start, axis=1, keepdims=True)
    tracer = (iota((COLS, COLS), 0) % (COLS // 2)) // REACH
    lane = iota((COLS, COLS), 1)
    total = base[...]
    for part in split(values):
        part = part.astype(F32)
        rows = [jnp.where(lane == tracer + i * SLOT, part, 0.0).astype(BF16) for i in range(2)]
        total += dot(picked_edge[...], jnp.concatenate(rows, axis=0))
    sent[...] = total


def main_kernel(fields, before, after, near, far, ops, scale, count, out, halo, dyn):
    halo[...] = halo_rows(before, after).astype(F32).T.astype(BF16)
    empty = jnp.zeros((TILE, COLS), BF16)
    for q in range(TRACERS):
        tiles = [empty] * (COLS // TILE)
        tiles[q // TURNS] = far[0, q % TURNS]
        tiles[COLS // TILE // 2 + q // TURNS] = far[1, q % TURNS]
        both = jnp.concatenate([fields[q], halo[...]], axis=1)
        summed = dot(both, jnp.concatenate([near[...], *tiles], axis=0))
        dyn[q] = (MIX * summed).astype(BF16)

    count2 = jnp.concatenate([count[...], count[...]], axis=1).astype(BF16)
    pairs = GROUP // 2

    def begin(base, p):
        return jnp.concatenate([dyn[base + 2 * p], dyn[base + 2 * p + 1]], axis=1)

    def group(g, carry):
        base = g * GROUP
        state = [begin(base, p) for p in range(pairs)]
        for s in range(KMAX):
            for p in range(pairs):
                both = dot(ops[s], state[p])
                tiles = []
                for t in range(LEVELS // TILE):
                    flat = both[2 * t * TILE : (2 * t + 1) * TILE]
                    bent = both[(2 * t + 1) * TILE : (2 * t + 2) * TILE]
                    factor = scale[t * TILE : (t + 1) * TILE]
                    factor = jnp.concatenate([factor, factor], axis=1)
                    tiles.append((flat + factor * bent).astype(BF16))
                widened = jnp.concatenate(tiles, axis=0)
                state[p] = widened if s == 0 else jnp.where(count2 > s, widened, state[p])
        for p in range(pairs):
            start = begin(base, p)
            result = start + (state[p] - start)
            for i in range(2):
                out[base + 2 * p + i] = result[:, i * COLS : (i + 1) * COLS]
        return carry

    lax.fori_loop(0, TRACERS // GROUP, group, 0)


def order_kernel(received, out):
    values = received[...]
    place = iota((COLS, COLS), 0)
    here = iota((COLS, COLS), 1)
    flags = values.astype(BF16)
    earlier = dot((here < place).astype(BF16), flags)
    first = values[:, TRACERS : TRACERS + 1]
    second = values[:, SLOT + TRACERS : SLOT + TRACERS + 1]
    rank = earlier[:, TRACERS : TRACERS + 1] + earlier[:, SLOT + TRACERS : SLOT + TRACERS + 1]
    spot = here.astype(F32)
    chosen = jnp.concatenate(
        [
            jnp.where(spot == rank, first, 0.0),
            jnp.where(spot == rank + first, second, 0.0),
        ],
        axis=0,
    ).astype(BF16)
    turned = values.T
    rows = jnp.concatenate([turned[:SLOT], turned[SLOT : 2 * SLOT]], axis=1)
    high, low = split(rows)
    out[...] = (dot(high, chosen) + dot(low, chosen))[:TRACERS]


def local(fields, neighbors, cost, dest, diffusivity, operators):
    size = lax.axis_size("narrow")
    up = [(i, (i + 1) % size) for i in range(size)]
    down = [(j, i) for i, j in up]
    flat = fields.reshape(TRACERS, LEVELS, COLS)
    vmem = pl.BlockSpec(memory_space=pltpu.VMEM)
    params = pltpu.CompilerParams(vmem_limit_bytes=ROOM)
    side = jax.ShapeDtypeStruct((SIDE, LEVELS), BF16)
    vmem = pl.BlockSpec(memory_space=pltpu.VMEM)
    params = pltpu.CompilerParams(vmem_limit_bytes=ROOM)
    meta = jnp.concatenate([neighbors.reshape(NEIGH, COLS), cost, dest, cost, dest], axis=0)
    left, right, own = pl.pallas_call(
        edge_kernel,
        out_shape=(side, side, jax.ShapeDtypeStruct((2 * COLS, LEVELS), BF16)),
        in_specs=[vmem],
        out_specs=[vmem] * 3,
        scratch_shapes=[
            pltpu.VMEM((SIDE, LEVELS), F32),
            pltpu.VMEM((SIDE, LEVELS), F32),
            pltpu.VMEM((NEAR * TRACERS, LEVELS), F32),
        ],
        compiler_params=params,
        cost_estimate=pl.CostEstimate(flops=2 * 10**9, bytes_accessed=4 * 10**6, transcendentals=0),
        name="edge",
    )(flat)
    before = lax.ppermute(right, "narrow", up)
    after = lax.ppermute(left, "narrow", down)
    square = jax.ShapeDtypeStruct((COLS, COLS), F32)
    square16 = jax.ShapeDtypeStruct((COLS, COLS), BF16)
    ops, near, far, scale, picked_edge, reach_edge, pull_edge, base_edge, count, base = pl.pallas_call(
        plan_kernel,
        out_shape=(
            jax.ShapeDtypeStruct((KMAX, 2 * LEVELS, LEVELS), BF16),
            square16,
            jax.ShapeDtypeStruct((2, TURNS, TILE, COLS), BF16),
            square,
            jax.ShapeDtypeStruct((COLS, 2 * COLS), BF16),
            square16,
            square,
            square,
            jax.ShapeDtypeStruct((1, COLS), F32),
            square,
        ),
        in_specs=[vmem] * 5,
        out_specs=[vmem] * 10,
        scratch_shapes=[
            pltpu.VMEM((KMAX, 2 * LEVELS, LEVELS), BF16),
            pltpu.VMEM((TRACERS, LEVELS, COLS), BF16),
            pltpu.VMEM((TRACERS, COLS), F32),
        ],
        compiler_params=params,
        cost_estimate=pl.CostEstimate(flops=10**7, bytes_accessed=10**6, transcendentals=0),
        name="plan",
    )(flat, own, meta, diffusivity.reshape(LEVELS, COLS), operators)
    sent = pl.pallas_call(
        start_kernel,
        out_shape=square,
        in_specs=[vmem] * 7,
        out_specs=vmem,
        compiler_params=params,
        name="start",
    )(before, after, picked_edge, reach_edge, pull_edge, base_edge, base)
    received = lax.all_to_all(sent, ("wide", "narrow"), split_axis=0, concat_axis=0, tiled=True)
    new = pl.pallas_call(
        main_kernel,
        out_shape=jax.ShapeDtypeStruct(flat.shape, BF16),
        in_specs=[vmem] * 8,
        out_specs=vmem,
        scratch_shapes=[
            pltpu.VMEM((LEVELS, COLS), BF16),
            pltpu.VMEM((TRACERS, LEVELS, COLS), BF16),
        ],
        compiler_params=params,
        cost_estimate=pl.CostEstimate(flops=10**10, bytes_accessed=10**7, transcendentals=0),
        name="physics",
    )(flat, before, after, near, far, ops, scale, count)
    burden = pl.pallas_call(
        order_kernel,
        out_shape=jax.ShapeDtypeStruct((TRACERS, COLS), F32),
        in_specs=[vmem],
        out_specs=vmem,
        compiler_params=params,
        name="order",
    )(received)
    return new.reshape(fields.shape), burden[None]


def solution(mesh):
    in_specs = (
        P(None, None, "wide", "narrow"),
        P(None, "wide", "narrow"),
        P("wide", "narrow"),
        P("wide", "narrow"),
        P(None, "wide", "narrow"),
        P(),
    )
    out_specs = (P(None, None, "wide", "narrow"), P(("wide", "narrow"), None, None))
    return jax.shard_map(local, mesh=mesh, in_specs=in_specs, out_specs=out_specs, check_vma=False)
```

time: 31.2 us -> 30.7 us (0.984)
  local copies, waits for them, and re-layouts: 1.78 us -> 1.17 us
  starting transfers between devices: 14 us -> 14.4 us
  Pallas kernels: 10.1 us -> 9.76 us
    pallas_call x1, Pallas kernels: 4.49 us -> 5.12 us  [local(): pl.pallas_call(main_kernel, out_shape=jax.ShapeDtypeStruct(flat.shape, BF...]
    unnamed x6 -> x14, local copies, waits for them, and re-layouts: 1.78 us -> 1.15 us
    pallas_call x2, Pallas kernels: 2.02 us -> 1.54 us  [the longest x1 1.03 us: local(): pl.pallas_call(start_kernel, out_shape=square, in_specs=[vmem] * 7, out_s...]
    pallas_call x1, Pallas kernels: 2.48 us -> 2.03 us  [local(): pl.pallas_call(plan_kernel, out_shape=(jax.ShapeDtypeStruct((KMAX, 2 * LE...]
    all_to_all x1, starting transfers between devices: 10.3 us -> 10.7 us  [local(): lax.all_to_all(sent, ('wide', 'narrow'), split_axis=0, concat_axis=0, til...]
  transfers between devices with their start and end apart: 3 -> 3, of which waited for: 1 -> 1; matrix products, arithmetic and copies ran while one was open for 0% -> 0% of each run, Pallas kernels for 22% -> 23%
where the time goes in v4:
time: 30.7 us; the launch traced here: 30.5 us
  starting transfers between devices  14.4 us (47%)
  Pallas kernels  9.76 us (32%)
  waiting for transfers between devices  4.48 us (15%)
  local copies, waits for them, and re-layouts  1.17 us (4%)
  between operations  0.7 us (2%)
    all_to_all x1, starting transfers between devices, local(): lax.all_to_all(sent, ('wide', 'narrow'), split_axis=0, concat_axis=0, til...  10.7 us
    pallas_call x1, Pallas kernels, local(): pl.pallas_call(main_kernel, out_shape=jax.ShapeDtypeStruct(flat.shape, BF...  5.12 us
    all_to_all x1, waiting for transfers between devices, local(): lax.all_to_all(sent, ('wide', 'narrow'), split_axis=0, concat_axis=0, til...  4.48 us
    ppermute x1, starting transfers between devices, local(): before = lax.ppermute(right, 'narrow', up)  2.16 us
    pallas_call x1, Pallas kernels, local(): pl.pallas_call(plan_kernel, out_shape=(jax.ShapeDtypeStruct((KMAX, 2 * LE...  2.03 us
    ppermute x1, starting transfers between devices, local(): after = lax.ppermute(left, 'narrow', down)  1.54 us
    unnamed x14, local copies, waits for them, and re-layouts  1.15 us
    pallas_call x1, Pallas kernels, local(): pl.pallas_call(order_kernel, out_shape=jax.ShapeDtypeStruct((TRACERS, COL...  1.07 us
  transfers between devices with their start and end apart: 3, of which 1 were waited for; matrix products, arithmetic and copies ran while one was open for 0% of the time, Pallas kernels for 23%

profile of v4, /device:TPU:1, one launch (start us, length us, event | category | flops | bytes accessed | tf_op | source)
XLA Modules:
  0.0 30.5 jit_solution(14401724744490574155)
XLA Ops:
  0.6 0.0 copy-start
  0.6 1.1 %copy-done = bf16[24,128,1,128]{3,1,2,0:T(8,128)(2,1)S(1)} copy-done((bf16[24,128,1,128]{3,1,2,0:T(8,128)(2,1)S(1)}, bf16[24,128,1,128]{3,1,2,0:T(8,128)(2,1)}, u32[]{:S(2)}) %copy-start) | copy-done | bytes 786456
  1.8 0.0 copy-start.1
  1.8 0.0 copy-start.2
  1.8 0.0 copy-start.3
  1.8 0.5 %edge.1 = (bf16[48,128]{1,0:T(8,128)(2,1)S(1)}, bf16[48,128]{1,0:T(8,128)(2,1)S(1)}, bf16[256,128]{1,0:T(8,128)(2,1)S(1)}) custom-call(bf16[24,128,128]{2,1,0:T(8,128)(2,1)S(1)} %bitcast.11), custom_call_target="tpu_custom_call" | custom-call | flops 2000000000 | bytes 4000000 | tf_op jit(solution)/shard_map/edge/pallas_call | solution.py:271
  2.3 0.0 copy-start.6
  2.3 2.2 %collective-permute-start = (bf16[48,128]{1,0:T(8,128)(2,1)S(1)}, bf16[48,128]{1,0:T(8,128)(2,1)S(1)}, u32[]{:S(2)}, u32[]{:S(2)}) collective-permute-start(bf16[48,128]{1,0:T(8,128)(2,1)S(1)} %get-tuple-element.15), channel_id=1, source_target_pairs={{0,1},{1,2},{2,3},{3,0},{4,5},{5,6},{6,7},{7,4},{8,9},{9,10},{10,1... | collective-permute-start | bytes 36872 | tf_op jit(solution)/shard_map/ppermute | solution.py:285
  4.4 0.0 copy-start.4
  4.4 0.0 copy-start.5
  4.4 1.5 %collective-permute-start.1 = (bf16[48,128]{1,0:T(8,128)(2,1)S(1)}, bf16[48,128]{1,0:T(8,128)(2,1)S(1)}, u32[]{:S(2)}, u32[]{:S(2)}) collective-permute-start(bf16[48,128]{1,0:T(8,128)(2,1)S(1)} %get-tuple-element.16), channel_id=1, source_target_pairs={{1,0},{2,1},{3,2},{0,3},{5,4},{6,5},{7,6},{4,7},{9,8},{10,9},{11,1... | collective-permute-start | bytes 36872 | tf_op jit(solution)/shard_map/ppermute | solution.py:286
  6.0 0.0 copy-done.6
  6.0 0.0 copy-done.4
  6.0 0.0 copy-done.5
  6.0 0.0 copy-done.1
  6.0 0.0 copy-done.2
  6.0 0.0 copy-done.3
  6.0 2.0 %plan.1 = (bf16[8,256,128]{2,1,0:T(8,128)(2,1)S(1)}, bf16[128,128]{1,0:T(8,128)(2,1)S(1)}, bf16[2,8,16,128]{3,2,1,0:T(8,128)(2,1)S(1)}, f32[128,128]{1,0:T(8,128...) custom-call(bf16[24,128,128]{2,1,0:T(8,128)(2,1)S(1)} %bitcast.12, ...), custom_call_target="tpu_custom_call" | custom-call | flops 10000000 | bytes 1000000 | tf_op jit(solution)/shard_map/plan/pallas_call | solution.py:289
  8.1 0.0 collective-permute-done.before
  8.1 0.0 collective-permute-done.1.after
  8.1 1.0 %start.1 = f32[128,128]{1,0:T(8,128)} custom-call(bf16[48,128]{1,0:T(8,128)(2,1)S(1)} %collective-permute-done.before, bf16[48,128]{1,0:T(8,128)(2,1)S(1)} %collective-permute-done.1.after, bf16[128,256]{1,0:T(8,128)(2,1)S(1)} %get-tuple-element.23.picked_edge, bf16[128,128]{1,0:T(8,128)(2,1)S(1)} %get-tuple-element.24.reach_edge, ...), custom_call_target="tpu_custom_call" | custom-call | tf_op jit(solution)/shard_map/start/pallas_call | solution.py:314
  9.1 10.7 %all-to-all-start = ((f32[128,1,128]{2,1,0:T(1,128)}), f32[128,1,128]{2,1,0:T(1,128)S(1)}, u32[]{:S(2)}, u32[]{:S(2)}) async-start(f32[128,1,128]{2,1,0:T(1,128)} %bitcast.6), calls=%async_computation | async-start | bytes 131072 | tf_op jit(solution)/shard_map/all_to_all | solution.py:322
  19.8 5.1 %physics.1 = bf16[24,128,128]{2,1,0:T(8,128)(2,1)} custom-call(bf16[24,128,128]{2,1,0:T(8,128)(2,1)S(1)} %bitcast.13, bf16[48,128]{1,0:T(8,128)(2,1)S(1)} %collective-permute-done.before, bf16[48,128]{1,0:T(8,128)(2,1)S(1)} %collective-permute-done.1.after, bf16[128,128]{1,0:T(8,128)(2,1)S(1)} %get-tuple-element.18.near, ...), custom_call_target="tpu_custom_call" | custom-call | flops 10000000000 | bytes 10000000 | tf_op jit(solution)/shard_map/physics/pallas_call | solution.py:323
  24.9 4.5 %all-to-all-done = f32[128,1,128]{2,1,0:T(1,128)S(1)} async-done(((f32[128,1,128]{2,1,0:T(1,128)}), f32[128,1,128]{2,1,0:T(1,128)S(1)}, u32[]{:S(2)}, u32[]{:S(2)}) %all-to-all-start) | async-done | bytes 65568 | tf_op jit(solution)/shard_map/all_to_all | solution.py:322
  29.4 1.1 %order.1 = f32[24,128]{1,0:T(8,128)} custom-call(f32[128,128]{1,0:T(8,128)S(1)} %bitcast.14), custom_call_target="tpu_custom_call" | custom-call | tf_op jit(solution)/shard_map/order/pallas_call | solution.py:336
  (1 shorter events, 0.0 us)
Async XLA Ops:
  0.6 1.1 %copy-start = (bf16[24,128,1,128]{3,1,2,0:T(8,128)(2,1)S(1)}, bf16[24,128,1,128]{3,1,2,0:T(8,128)(2,1)}, u32[]{:S(2)}) copy-start(bf16[24,128,1,128]{3,1,2,0:T(8,128)(2,1)} %param.6) | copy-start | bytes 2359300
  1.8 4.3 %copy-start.1 = (bf16[24,128,1,128]{3,1,2,0:T(8,128)(2,1)S(1)}, bf16[24,128,1,128]{3,1,2,0:T(8,128)(2,1)}, u32[]{:S(2)}) copy-start(bf16[24,128,1,128]{3,1,2,0:T(8,128)(2,1)} %param.6) | copy-start | bytes 2359300
  1.8 4.3 %copy-start.2 = (bf16[8,128,128]{2,1,0:T(8,128)(2,1)S(1)}, bf16[8,128,128]{2,1,0:T(8,128)(2,1)}, u32[]{:S(2)}) copy-start(bf16[8,128,128]{2,1,0:T(8,128)(2,1)} %operators.1) | copy-start | bytes 786436
  1.8 4.3 %copy-start.3 = (bf16[128,1,128]{2,0,1:T(8,128)(2,1)S(1)}, bf16[128,1,128]{2,0,1:T(8,128)(2,1)}, u32[]{:S(2)}) copy-start(bf16[128,1,128]{2,0,1:T(8,128)(2,1)} %param.10) | copy-start | bytes 98308
  2.3 3.7 %copy-start.6 = (s32[4,1,128]{2,1,0:T(1,128)S(1)}, s32[4,1,128]{2,1,0:T(1,128)}, u32[]{:S(2)}) copy-start(s32[4,1,128]{2,1,0:T(1,128)} %param.7) | copy-start | bytes 6148
  2.3 5.8 %collective-permute-start = (bf16[48,128]{1,0:T(8,128)(2,1)S(1)}, bf16[48,128]{1,0:T(8,128)(2,1)S(1)}, u32[]{:S(2)}, u32[]{:S(2)}) collective-permute-start(bf16[48,128]{1,0:T(8,128)(2,1)S(1)} %get-tuple-element.15), channel_id=1, source_target_pairs={{0,1},{1,2},{2,3},{3,0},{4,5},{5,6},{6,7},{7,4},{8,9},{9,10},{10,1... | collective-permute-start | bytes 36872 | tf_op jit(solution)/shard_map/ppermute | solution.py:285
  4.4 1.5 %copy-start.4 = (s32[1,128]{1,0:T(1,128)S(1)}, s32[1,128]{1,0:T(1,128)}, u32[]{:S(2)}) copy-start(s32[1,128]{1,0:T(1,128)} %param.8) | copy-start | bytes 1540
  4.4 1.6 %copy-start.5 = (s32[1,128]{1,0:T(1,128)S(1)}, s32[1,128]{1,0:T(1,128)}, u32[]{:S(2)}) copy-start(s32[1,128]{1,0:T(1,128)} %param.9) | copy-start | bytes 1540
  4.4 3.6 %collective-permute-start.1 = (bf16[48,128]{1,0:T(8,128)(2,1)S(1)}, bf16[48,128]{1,0:T(8,128)(2,1)S(1)}, u32[]{:S(2)}, u32[]{:S(2)}) collective-permute-start(bf16[48,128]{1,0:T(8,128)(2,1)S(1)} %get-tuple-element.16), channel_id=1, source_target_pairs={{1,0},{2,1},{3,2},{0,3},{5,4},{6,5},{7,6},{4,7},{9,8},{10,9},{11,1... | collective-permute-start | bytes 36872 | tf_op jit(solution)/shard_map/ppermute | solution.py:286
  9.1 20.3 %all-to-all-start = ((f32[128,1,128]{2,1,0:T(1,128)}), f32[128,1,128]{2,1,0:T(1,128)S(1)}, u32[]{:S(2)}, u32[]{:S(2)}) async-start(f32[128,1,128]{2,1,0:T(1,128)} %bitcast.6), calls=%async_computation | async-start | bytes 131072 | tf_op jit(solution)/shard_map/all_to_all | solution.py:322

commit v5 on v4

--- a/solution.py
+++ b/solution.py
@@ -203,7 +203,7 @@
         summed = dot(both, jnp.concatenate([near[...], *tiles], axis=0))
         dyn[q] = (MIX * summed).astype(BF16)
 
-    count2 = jnp.concatenate([count[...], count[...]], axis=1).astype(BF16)
+    count2 = jnp.concatenate([count[...], count[...]], axis=1)
     pairs = GROUP // 2
 
     def begin(base, p):
@@ -212,21 +212,24 @@
     def group(g, carry):
         base = g * GROUP
         state = [begin(base, p) for p in range(pairs)]
+        final = [None] * pairs
         for s in range(KMAX):
             for p in range(pairs):
                 both = dot(ops[s], state[p])
-                tiles = []
+                tiles, lasts = [], []
                 for t in range(LEVELS // TILE):
                     flat = both[2 * t * TILE : (2 * t + 1) * TILE]
                     bent = both[(2 * t + 1) * TILE : (2 * t + 2) * TILE]
                     factor = scale[t * TILE : (t + 1) * TILE]
                     factor = jnp.concatenate([factor, factor], axis=1)
-                    tiles.append((flat + factor * bent).astype(BF16))
-                widened = jnp.concatenate(tiles, axis=0)
-                state[p] = widened if s == 0 else jnp.where(count2 > s, widened, state[p])
+                    widened = flat + factor * bent
+                    tiles.append(widened.astype(BF16))
+                    lasts.append(widened if s == 0 else jnp.where(count2 > s, widened, final[p][t]))
+                state[p], final[p] = jnp.concatenate(tiles, axis=0), lasts
         for p in range(pairs):
-            start = begin(base, p)
-            result = start + (state[p] - start)
+            start = begin(base, p).astype(F32)
+            tend = (jnp.concatenate(final[p], axis=0) - start).astype(BF16)
+            result = (start + tend.astype(F32)).astype(BF16)
             for i in range(2):
                 out[base + 2 * p + i] = result[:, i * COLS : (i + 1) * COLS]
         return carry

time: 30.7 us -> 30.7 us (level)
  transfers between devices with their start and end apart: 3 -> 3, of which waited for: 1 -> 1; matrix products, arithmetic and copies ran while one was open for 0% -> 0% of each run, Pallas kernels for 23% -> 24%
where the time goes in v5:
time: 30.7 us; the launch traced here: 30.5 us
  starting transfers between devices  14.4 us (47%)
  Pallas kernels  9.8 us (32%)
  waiting for transfers between devices  4.44 us (14%)
  local copies, waits for them, and re-layouts  1.17 us (4%)
  between operations  0.7 us (2%)
    all_to_all x1, starting transfers between devices, local(): lax.all_to_all(sent, ('wide', 'narrow'), split_axis=0, concat_axis=0, til...  10.7 us
    pallas_call x1, Pallas kernels, local(): pl.pallas_call(main_kernel, out_shape=jax.ShapeDtypeStruct(flat.shape, BF...  5.16 us
    all_to_all x1, waiting for transfers between devices, local(): lax.all_to_all(sent, ('wide', 'narrow'), split_axis=0, concat_axis=0, til...  4.44 us
    ppermute x1, starting transfers between devices, local(): before = lax.ppermute(right, 'narrow', up)  2.16 us
    pallas_call x1, Pallas kernels, local(): pl.pallas_call(plan_kernel, out_shape=(jax.ShapeDtypeStruct((KMAX, 2 * LE...  2.03 us
    ppermute x1, starting transfers between devices, local(): after = lax.ppermute(left, 'narrow', down)  1.54 us
    unnamed x14, local copies, waits for them, and re-layouts  1.15 us
    pallas_call x1, Pallas kernels, local(): pl.pallas_call(order_kernel, out_shape=jax.ShapeDtypeStruct((TRACERS, COL...  1.07 us
  transfers between devices with their start and end apart: 3, of which 1 were waited for; matrix products, arithmetic and copies ran while one was open for 0% of the time, Pallas kernels for 24%

profile of v5, /device:TPU:1, one launch (start us, length us, event | category | flops | bytes accessed | tf_op | source)
XLA Modules:
  0.0 30.5 jit_solution(11301986307874848102)
XLA Ops:
  0.6 0.0 copy-start
  0.6 1.1 %copy-done = bf16[24,128,1,128]{3,1,2,0:T(8,128)(2,1)S(1)} copy-done((bf16[24,128,1,128]{3,1,2,0:T(8,128)(2,1)S(1)}, bf16[24,128,1,128]{3,1,2,0:T(8,128)(2,1)}, u32[]{:S(2)}) %copy-start) | copy-done | bytes 786456
  1.8 0.0 copy-start.1
  1.8 0.0 copy-start.2
  1.8 0.0 copy-start.3
  1.8 0.5 %edge.1 = (bf16[48,128]{1,0:T(8,128)(2,1)S(1)}, bf16[48,128]{1,0:T(8,128)(2,1)S(1)}, bf16[256,128]{1,0:T(8,128)(2,1)S(1)}) custom-call(bf16[24,128,128]{2,1,0:T(8,128)(2,1)S(1)} %bitcast.11), custom_call_target="tpu_custom_call" | custom-call | flops 2000000000 | bytes 4000000 | tf_op jit(solution)/shard_map/edge/pallas_call | solution.py:274
  2.3 0.0 copy-start.6
  2.3 2.2 %collective-permute-start = (bf16[48,128]{1,0:T(8,128)(2,1)S(1)}, bf16[48,128]{1,0:T(8,128)(2,1)S(1)}, u32[]{:S(2)}, u32[]{:S(2)}) collective-permute-start(bf16[48,128]{1,0:T(8,128)(2,1)S(1)} %get-tuple-element.15), channel_id=1, source_target_pairs={{0,1},{1,2},{2,3},{3,0},{4,5},{5,6},{6,7},{7,4},{8,9},{9,10},{10,1... | collective-permute-start | bytes 36872 | tf_op jit(solution)/shard_map/ppermute | solution.py:288
  4.4 0.0 copy-start.4
  4.4 0.0 copy-start.5
  4.4 1.5 %collective-permute-start.1 = (bf16[48,128]{1,0:T(8,128)(2,1)S(1)}, bf16[48,128]{1,0:T(8,128)(2,1)S(1)}, u32[]{:S(2)}, u32[]{:S(2)}) collective-permute-start(bf16[48,128]{1,0:T(8,128)(2,1)S(1)} %get-tuple-element.16), channel_id=1, source_target_pairs={{1,0},{2,1},{3,2},{0,3},{5,4},{6,5},{7,6},{4,7},{9,8},{10,9},{11,1... | collective-permute-start | bytes 36872 | tf_op jit(solution)/shard_map/ppermute | solution.py:289
  6.0 0.0 copy-done.6
  6.0 0.0 copy-done.4
  6.0 0.0 copy-done.5
  6.0 0.0 copy-done.1
  6.0 0.0 copy-done.2
  6.0 0.0 copy-done.3
  6.0 2.0 %plan.1 = (bf16[8,256,128]{2,1,0:T(8,128)(2,1)S(1)}, bf16[128,128]{1,0:T(8,128)(2,1)S(1)}, bf16[2,8,16,128]{3,2,1,0:T(8,128)(2,1)S(1)}, f32[128,128]{1,0:T(8,128...) custom-call(bf16[24,128,128]{2,1,0:T(8,128)(2,1)S(1)} %bitcast.12, ...), custom_call_target="tpu_custom_call" | custom-call | flops 10000000 | bytes 1000000 | tf_op jit(solution)/shard_map/plan/pallas_call | solution.py:292
  8.1 0.0 collective-permute-done.before
  8.1 0.0 collective-permute-done.1.after
  8.1 1.0 %start.1 = f32[128,128]{1,0:T(8,128)} custom-call(bf16[48,128]{1,0:T(8,128)(2,1)S(1)} %collective-permute-done.before, bf16[48,128]{1,0:T(8,128)(2,1)S(1)} %collective-permute-done.1.after, bf16[128,256]{1,0:T(8,128)(2,1)S(1)} %get-tuple-element.23.picked_edge, bf16[128,128]{1,0:T(8,128)(2,1)S(1)} %get-tuple-element.24.reach_edge, ...), custom_call_target="tpu_custom_call" | custom-call | tf_op jit(solution)/shard_map/start/pallas_call | solution.py:317
  9.1 10.7 %all-to-all-start = ((f32[128,1,128]{2,1,0:T(1,128)}), f32[128,1,128]{2,1,0:T(1,128)S(1)}, u32[]{:S(2)}, u32[]{:S(2)}) async-start(f32[128,1,128]{2,1,0:T(1,128)} %bitcast.6), calls=%async_computation | async-start | bytes 131072 | tf_op jit(solution)/shard_map/all_to_all | solution.py:325
  19.8 5.2 %physics.1 = bf16[24,128,128]{2,1,0:T(8,128)(2,1)} custom-call(bf16[24,128,128]{2,1,0:T(8,128)(2,1)S(1)} %bitcast.13, bf16[48,128]{1,0:T(8,128)(2,1)S(1)} %collective-permute-done.before, bf16[48,128]{1,0:T(8,128)(2,1)S(1)} %collective-permute-done.1.after, bf16[128,128]{1,0:T(8,128)(2,1)S(1)} %get-tuple-element.18.near, ...), custom_call_target="tpu_custom_call" | custom-call | flops 10000000000 | bytes 10000000 | tf_op jit(solution)/shard_map/physics/pallas_call | solution.py:326
  25.0 4.4 %all-to-all-done = f32[128,1,128]{2,1,0:T(1,128)S(1)} async-done(((f32[128,1,128]{2,1,0:T(1,128)}), f32[128,1,128]{2,1,0:T(1,128)S(1)}, u32[]{:S(2)}, u32[]{:S(2)}) %all-to-all-start) | async-done | bytes 65568 | tf_op jit(solution)/shard_map/all_to_all | solution.py:325
  29.4 1.1 %order.1 = f32[24,128]{1,0:T(8,128)} custom-call(f32[128,128]{1,0:T(8,128)S(1)} %bitcast.14), custom_call_target="tpu_custom_call" | custom-call | tf_op jit(solution)/shard_map/order/pallas_call | solution.py:339
  (1 shorter events, 0.0 us)
Async XLA Ops:
  0.6 1.1 %copy-start = (bf16[24,128,1,128]{3,1,2,0:T(8,128)(2,1)S(1)}, bf16[24,128,1,128]{3,1,2,0:T(8,128)(2,1)}, u32[]{:S(2)}) copy-start(bf16[24,128,1,128]{3,1,2,0:T(8,128)(2,1)} %param.6) | copy-start | bytes 2359300
  1.8 4.3 %copy-start.1 = (bf16[24,128,1,128]{3,1,2,0:T(8,128)(2,1)S(1)}, bf16[24,128,1,128]{3,1,2,0:T(8,128)(2,1)}, u32[]{:S(2)}) copy-start(bf16[24,128,1,128]{3,1,2,0:T(8,128)(2,1)} %param.6) | copy-start | bytes 2359300
  1.8 4.3 %copy-start.2 = (bf16[8,128,128]{2,1,0:T(8,128)(2,1)S(1)}, bf16[8,128,128]{2,1,0:T(8,128)(2,1)}, u32[]{:S(2)}) copy-start(bf16[8,128,128]{2,1,0:T(8,128)(2,1)} %operators.1) | copy-start | bytes 786436
  1.8 4.3 %copy-start.3 = (bf16[128,1,128]{2,0,1:T(8,128)(2,1)S(1)}, bf16[128,1,128]{2,0,1:T(8,128)(2,1)}, u32[]{:S(2)}) copy-start(bf16[128,1,128]{2,0,1:T(8,128)(2,1)} %param.10) | copy-start | bytes 98308
  2.3 3.7 %copy-start.6 = (s32[4,1,128]{2,1,0:T(1,128)S(1)}, s32[4,1,128]{2,1,0:T(1,128)}, u32[]{:S(2)}) copy-start(s32[4,1,128]{2,1,0:T(1,128)} %param.7) | copy-start | bytes 6148
  2.3 5.8 %collective-permute-start = (bf16[48,128]{1,0:T(8,128)(2,1)S(1)}, bf16[48,128]{1,0:T(8,128)(2,1)S(1)}, u32[]{:S(2)}, u32[]{:S(2)}) collective-permute-start(bf16[48,128]{1,0:T(8,128)(2,1)S(1)} %get-tuple-element.15), channel_id=1, source_target_pairs={{0,1},{1,2},{2,3},{3,0},{4,5},{5,6},{6,7},{7,4},{8,9},{9,10},{10,1... | collective-permute-start | bytes 36872 | tf_op jit(solution)/shard_map/ppermute | solution.py:288
  4.4 1.5 %copy-start.4 = (s32[1,128]{1,0:T(1,128)S(1)}, s32[1,128]{1,0:T(1,128)}, u32[]{:S(2)}) copy-start(s32[1,128]{1,0:T(1,128)} %param.8) | copy-start | bytes 1540
  4.4 1.6 %copy-start.5 = (s32[1,128]{1,0:T(1,128)S(1)}, s32[1,128]{1,0:T(1,128)}, u32[]{:S(2)}) copy-start(s32[1,128]{1,0:T(1,128)} %param.9) | copy-start | bytes 1540
  4.4 3.6 %collective-permute-start.1 = (bf16[48,128]{1,0:T(8,128)(2,1)S(1)}, bf16[48,128]{1,0:T(8,128)(2,1)S(1)}, u32[]{:S(2)}, u32[]{:S(2)}) collective-permute-start(bf16[48,128]{1,0:T(8,128)(2,1)S(1)} %get-tuple-element.16), channel_id=1, source_target_pairs={{1,0},{2,1},{3,2},{0,3},{5,4},{6,5},{7,6},{4,7},{9,8},{10,9},{11,1... | collective-permute-start | bytes 36872 | tf_op jit(solution)/shard_map/ppermute | solution.py:289
  9.1 20.3 %all-to-all-start = ((f32[128,1,128]{2,1,0:T(1,128)}), f32[128,1,128]{2,1,0:T(1,128)S(1)}, u32[]{:S(2)}, u32[]{:S(2)}) async-start(f32[128,1,128]{2,1,0:T(1,128)} %bitcast.6), calls=%async_computation | async-start | bytes 131072 | tf_op jit(solution)/shard_map/all_to_all | solution.py:325

commit v6 on v5

--- a/solution.py
+++ b/solution.py
@@ -262,8 +262,8 @@
 
 def local(fields, neighbors, cost, dest, diffusivity, operators):
     size = lax.axis_size("narrow")
-    up = [(i, (i + 1) % size) for i in range(size)]
-    down = [(j, i) for i, j in up]
+    odd = lax.axis_index("narrow") % 2 == 1
+    trades = [[(i, (i + 1 if i % 2 == turn else i - 1) % size) for i in range(size)] for turn in (1, 0)]
     flat = fields.reshape(TRACERS, LEVELS, COLS)
     vmem = pl.BlockSpec(memory_space=pltpu.VMEM)
     params = pltpu.CompilerParams(vmem_limit_bytes=ROOM)
@@ -285,8 +285,10 @@
         cost_estimate=pl.CostEstimate(flops=2 * 10**9, bytes_accessed=4 * 10**6, transcendentals=0),
         name="edge",
     )(flat)
-    before = lax.ppermute(right, "narrow", up)
-    after = lax.ppermute(left, "narrow", down)
+    first = lax.ppermute(jnp.where(odd, right, left), "narrow", trades[0])
+    second = lax.ppermute(jnp.where(odd, left, right), "narrow", trades[1])
+    before = jnp.where(odd, second, first)
+    after = jnp.where(odd, first, second)
     square = jax.ShapeDtypeStruct((COLS, COLS), F32)
     square16 = jax.ShapeDtypeStruct((COLS, COLS), BF16)
     ops, near, far, scale, picked_edge, reach_edge, pull_edge, base_edge, count, base = pl.pallas_call(

time: 30.7 us -> 30.6 us (level)
  starting transfers between devices: 14.4 us -> 13.5 us
  local copies, waits for them, and re-layouts: 1.17 us -> 1.83 us
    all_to_all x1, starting transfers between devices: 10.7 us -> 9.89 us  [local(): lax.all_to_all(sent, ('wide', 'narrow'), split_axis=0, concat_axis=0, til...]
    unnamed x14, local copies, waits for them, and re-layouts: 1.15 us -> 1.8 us
where the time goes in v6:
time: 30.6 us; the launch traced here: 30.4 us
  starting transfers between devices  13.5 us (44%)
  Pallas kernels  9.77 us (32%)
  waiting for transfers between devices  4.51 us (15%)
  local copies, waits for them, and re-layouts  1.83 us (6%)
  between operations  0.73 us (2%)
    all_to_all x1, starting transfers between devices, local(): lax.all_to_all(sent, ('wide', 'narrow'), split_axis=0, concat_axis=0, til...  9.89 us
    pallas_call x1, Pallas kernels, local(): pl.pallas_call(main_kernel, out_shape=jax.ShapeDtypeStruct(flat.shape, BF...  5.16 us
    all_to_all x1, waiting for transfers between devices, local(): lax.all_to_all(sent, ('wide', 'narrow'), split_axis=0, concat_axis=0, til...  4.51 us
    ppermute x1, starting transfers between devices, local(): first = lax.ppermute(jnp.where(odd, right, left), 'narrow', trades[0])  3.63 us
    pallas_call x1, Pallas kernels, local(): pl.pallas_call(plan_kernel, out_shape=(jax.ShapeDtypeStruct((KMAX, 2 * LE...  2.02 us
    unnamed x14, local copies, waits for them, and re-layouts  1.8 us
    pallas_call x1, Pallas kernels, local(): pl.pallas_call(order_kernel, out_shape=jax.ShapeDtypeStruct((TRACERS, COL...  1.07 us
    pallas_call x1, Pallas kernels, local(): pl.pallas_call(start_kernel, out_shape=square, in_specs=[vmem] * 7, out_s...  1.01 us
  transfers between devices with their start and end apart: 3, of which 1 were waited for; matrix products, arithmetic and copies ran while one was open for 0% of the time, Pallas kernels for 24%

profile of v6, /device:TPU:1, one launch (start us, length us, event | category | flops | bytes accessed | tf_op | source)
XLA Modules:
  0.0 30.4 jit_solution(764740002828402156)
XLA Ops:
  0.6 0.0 copy-start
  0.7 1.1 %copy-done = bf16[24,128,1,128]{3,1,2,0:T(8,128)(2,1)S(1)} copy-done((bf16[24,128,1,128]{3,1,2,0:T(8,128)(2,1)S(1)}, bf16[24,128,1,128]{3,1,2,0:T(8,128)(2,1)}, u32[]{:S(2)}) %copy-start) | copy-done | bytes 786456
  1.8 0.0 copy-start.1
  1.8 0.0 copy-start.2
  1.8 0.5 %edge.1 = (bf16[48,128]{1,0:T(8,128)(2,1)S(1)}, bf16[48,128]{1,0:T(8,128)(2,1)S(1)}, bf16[256,128]{1,0:T(8,128)(2,1)S(1)}) custom-call(bf16[24,128,128]{2,1,0:T(8,128)(2,1)S(1)} %bitcast.11), custom_call_target="tpu_custom_call" | custom-call | flops 2000000000 | bytes 4000000 | tf_op jit(solution)/shard_map/edge/pallas_call | solution.py:274
  2.3 0.0 copy-start.3
  2.3 0.0 copy-start.6
  2.3 3.6 %collective-permute-start.1 = (bf16[48,128]{1,0:T(8,128)(2,1)S(1)}, bf16[48,128]{1,0:T(8,128)(2,1)S(1)}, u32[]{:S(2)}, u32[]{:S(2)}) collective-permute-start(bf16[48,128]{1,0:T(8,128)(2,1)S(1)} %get-tuple-element.34), channel_id=1, source_target_pairs={{0,3},{1,2},{2,1},{3,0},{4,7},{5,6},{6,5},{7,4},{8,11},{9,10},{10,... | collective-permute-start | bytes 36872 | tf_op jit(solution)/shard_map/ppermute | solution.py:288
  6.0 0.0 copy-start.4
  6.0 0.0 copy-start.5
  6.0 0.0 collective-permute-start
  6.0 0.0 copy-done.6
  6.0 0.6 %copy-done.4 = s32[1,128]{1,0:T(1,128)S(1)} copy-done((s32[1,128]{1,0:T(1,128)S(1)}, s32[1,128]{1,0:T(1,128)}, u32[]{:S(2)}) %copy-start.4) | copy-done | bytes 536
  6.6 0.0 copy-done.5
  6.7 0.0 copy-done.1
  6.7 0.0 copy-done.2
  6.7 0.0 copy-done.3
  6.7 2.0 %plan.1 = (bf16[8,256,128]{2,1,0:T(8,128)(2,1)S(1)}, bf16[128,128]{1,0:T(8,128)(2,1)S(1)}, bf16[2,8,16,128]{3,2,1,0:T(8,128)(2,1)S(1)}, f32[128,128]{1,0:T(8,128...) custom-call(bf16[24,128,128]{2,1,0:T(8,128)(2,1)S(1)} %bitcast.12, ...), custom_call_target="tpu_custom_call" | custom-call | flops 10000000 | bytes 1000000 | tf_op jit(solution)/shard_map/plan/pallas_call | solution.py:294
  8.7 0.0 collective-permute-done.1
  8.7 0.0 collective-permute-done
  8.7 1.0 %start.1 = f32[128,128]{1,0:T(8,128)} custom-call(bf16[48,128]{1,0:T(8,128)(2,1)S(1)} %get-tuple-element.33.before, bf16[48,128]{1,0:T(8,128)(2,1)S(1)} %get-tuple-element.32.after, bf16[128,256]{1,0:T(8,128)(2,1)S(1)} %get-tuple-element.23.picked_edge, bf16[128,128]{1,0:T(8,128)(2,1)S(1)} %get-tuple-element.24.reach_edge, ...), custom_call_target="tpu_custom_call" | custom-call | tf_op jit(solution)/shard_map/start/pallas_call | solution.py:319
  9.8 9.9 %all-to-all-start = ((f32[128,1,128]{2,1,0:T(1,128)}), f32[128,1,128]{2,1,0:T(1,128)S(1)}, u32[]{:S(2)}, u32[]{:S(2)}) async-start(f32[128,1,128]{2,1,0:T(1,128)} %bitcast.6), calls=%async_computation | async-start | bytes 131072 | tf_op jit(solution)/shard_map/all_to_all | solution.py:327
  19.7 5.2 %physics.1 = bf16[24,128,128]{2,1,0:T(8,128)(2,1)} custom-call(bf16[24,128,128]{2,1,0:T(8,128)(2,1)S(1)} %bitcast.13, bf16[48,128]{1,0:T(8,128)(2,1)S(1)} %get-tuple-element.33.before, bf16[48,128]{1,0:T(8,128)(2,1)S(1)} %get-tuple-element.32.after, bf16[128,128]{1,0:T(8,128)(2,1)S(1)} %get-tuple-element.18.near, ...), custom_call_target="tpu_custom_call" | custom-call | flops 10000000000 | bytes 10000000 | tf_op jit(solution)/shard_map/physics/pallas_call | solution.py:328
  24.8 4.5 %all-to-all-done = f32[128,1,128]{2,1,0:T(1,128)S(1)} async-done(((f32[128,1,128]{2,1,0:T(1,128)}), f32[128,1,128]{2,1,0:T(1,128)S(1)}, u32[]{:S(2)}, u32[]{:S(2)}) %all-to-all-start) | async-done | bytes 65568 | tf_op jit(solution)/shard_map/all_to_all | solution.py:327
  29.3 1.1 %order.1 = f32[24,128]{1,0:T(8,128)} custom-call(f32[128,128]{1,0:T(8,128)S(1)} %bitcast.14), custom_call_target="tpu_custom_call" | custom-call | tf_op jit(solution)/shard_map/order/pallas_call | solution.py:341
  (3 shorter events, 0.0 us)
Async XLA Ops:
  0.6 1.1 %copy-start = (bf16[24,128,1,128]{3,1,2,0:T(8,128)(2,1)S(1)}, bf16[24,128,1,128]{3,1,2,0:T(8,128)(2,1)}, u32[]{:S(2)}) copy-start(bf16[24,128,1,128]{3,1,2,0:T(8,128)(2,1)} %param.6) | copy-start | bytes 2359300
  1.8 4.9 %copy-start.1 = (bf16[24,128,1,128]{3,1,2,0:T(8,128)(2,1)S(1)}, bf16[24,128,1,128]{3,1,2,0:T(8,128)(2,1)}, u32[]{:S(2)}) copy-start(bf16[24,128,1,128]{3,1,2,0:T(8,128)(2,1)} %param.6) | copy-start | bytes 2359300
  1.8 4.9 %copy-start.2 = (bf16[8,128,128]{2,1,0:T(8,128)(2,1)S(1)}, bf16[8,128,128]{2,1,0:T(8,128)(2,1)}, u32[]{:S(2)}) copy-start(bf16[8,128,128]{2,1,0:T(8,128)(2,1)} %operators.1) | copy-start | bytes 786436
  2.3 4.4 %copy-start.3 = (bf16[128,1,128]{2,0,1:T(8,128)(2,1)S(1)}, bf16[128,1,128]{2,0,1:T(8,128)(2,1)}, u32[]{:S(2)}) copy-start(bf16[128,1,128]{2,0,1:T(8,128)(2,1)} %param.10) | copy-start | bytes 98308
  2.3 3.7 %copy-start.6 = (s32[4,1,128]{2,1,0:T(1,128)S(1)}, s32[4,1,128]{2,1,0:T(1,128)}, u32[]{:S(2)}) copy-start(s32[4,1,128]{2,1,0:T(1,128)} %param.7) | copy-start | bytes 6148
  2.3 6.4 %collective-permute-start.1 = (bf16[48,128]{1,0:T(8,128)(2,1)S(1)}, bf16[48,128]{1,0:T(8,128)(2,1)S(1)}, u32[]{:S(2)}, u32[]{:S(2)}) collective-permute-start(bf16[48,128]{1,0:T(8,128)(2,1)S(1)} %get-tuple-element.34), channel_id=1, source_target_pairs={{0,3},{1,2},{2,1},{3,0},{4,7},{5,6},{6,5},{7,4},{8,11},{9,10},{10,... | collective-permute-start | bytes 36872 | tf_op jit(solution)/shard_map/ppermute | solution.py:288
  6.0 0.7 %copy-start.4 = (s32[1,128]{1,0:T(1,128)S(1)}, s32[1,128]{1,0:T(1,128)}, u32[]{:S(2)}) copy-start(s32[1,128]{1,0:T(1,128)} %param.8) | copy-start | bytes 1540
  6.0 0.7 %copy-start.5 = (s32[1,128]{1,0:T(1,128)S(1)}, s32[1,128]{1,0:T(1,128)}, u32[]{:S(2)}) copy-start(s32[1,128]{1,0:T(1,128)} %param.9) | copy-start | bytes 1540
  6.0 2.8 %collective-permute-start = (bf16[48,128]{1,0:T(8,128)(2,1)S(1)}, bf16[48,128]{1,0:T(8,128)(2,1)S(1)}, u32[]{:S(2)}, u32[]{:S(2)}) collective-permute-start(bf16[48,128]{1,0:T(8,128)(2,1)S(1)} %get-tuple-element.35), channel_id=1, source_target_pairs={{0,1},{1,0},{2,3},{3,2},{4,5},{5,4},{6,7},{7,6},{8,9},{9,8},{10,11... | collective-permute-start | bytes 36872 | tf_op jit(solution)/shard_map/ppermute | solution.py:289
  9.8 19.6 %all-to-all-start = ((f32[128,1,128]{2,1,0:T(1,128)}), f32[128,1,128]{2,1,0:T(1,128)S(1)}, u32[]{:S(2)}, u32[]{:S(2)}) async-start(f32[128,1,128]{2,1,0:T(1,128)} %bitcast.6), calls=%async_computation | async-start | bytes 131072 | tf_op jit(solution)/shard_map/all_to_all | solution.py:327

commit v7 on v5

--- a/solution.py
+++ b/solution.py
@@ -184,12 +184,13 @@
     values = jnp.sum(pull_edge[...] * start, axis=1, keepdims=True)
     tracer = (iota((COLS, COLS), 0) % (COLS // 2)) // REACH
     lane = iota((COLS, COLS), 1)
-    total = base[...]
+    parts = []
     for part in split(values):
         part = part.astype(F32)
         rows = [jnp.where(lane == tracer + i * SLOT, part, 0.0).astype(BF16) for i in range(2)]
-        total += dot(picked_edge[...], jnp.concatenate(rows, axis=0))
-    sent[...] = total
+        parts.append(jnp.concatenate(rows, axis=0))
+    moved = dot(picked_edge[...], jnp.concatenate(parts, axis=1))
+    sent[...] = base[...] + moved[:, :COLS] + moved[:, COLS:]
 
 
 def main_kernel(fields, before, after, near, far, ops, scale, count, out, halo, dyn):
@@ -257,7 +258,8 @@
     turned = values.T
     rows = jnp.concatenate([turned[:SLOT], turned[SLOT : 2 * SLOT]], axis=1)
     high, low = split(rows)
-    out[...] = (dot(high, chosen) + dot(low, chosen))[:TRACERS]
+    moved = dot(jnp.concatenate([high, low], axis=0), chosen)
+    out[...] = moved[:TRACERS] + moved[SLOT : SLOT + TRACERS]
 
 
 def local(fields, neighbors, cost, dest, diffusivity, operators):

time: 30.7 us -> 30.7 us (level)
  no operation moved by 1% of the time
where the time goes in v7:
time: 30.7 us; the launch traced here: 30.5 us
  starting transfers between devices  14.4 us (47%)
  Pallas kernels  9.79 us (32%)
  waiting for transfers between devices  4.44 us (14%)
  local copies, waits for them, and re-layouts  1.17 us (4%)
  between operations  0.7 us (2%)
    all_to_all x1, starting transfers between devices, local(): lax.all_to_all(sent, ('wide', 'narrow'), split_axis=0, concat_axis=0, til...  10.7 us
    pallas_call x1, Pallas kernels, local(): pl.pallas_call(main_kernel, out_shape=jax.ShapeDtypeStruct(flat.shape, BF...  5.16 us
    all_to_all x1, waiting for transfers between devices, local(): lax.all_to_all(sent, ('wide', 'narrow'), split_axis=0, concat_axis=0, til...  4.43 us
    ppermute x1, starting transfers between devices, local(): before = lax.ppermute(right, 'narrow', up)  2.16 us
    pallas_call x1, Pallas kernels, local(): pl.pallas_call(plan_kernel, out_shape=(jax.ShapeDtypeStruct((KMAX, 2 * LE...  2.03 us
    ppermute x1, starting transfers between devices, local(): after = lax.ppermute(left, 'narrow', down)  1.54 us
    unnamed x14, local copies, waits for them, and re-layouts  1.15 us
    pallas_call x1, Pallas kernels, local(): pl.pallas_call(order_kernel, out_shape=jax.ShapeDtypeStruct((TRACERS, COL...  1.06 us
  transfers between devices with their start and end apart: 3, of which 1 were waited for; matrix products, arithmetic and copies ran while one was open for 0% of the time, Pallas kernels for 24%

profile of v7, /device:TPU:1, one launch (start us, length us, event | category | flops | bytes accessed | tf_op | source)
XLA Modules:
  0.0 30.5 jit_solution(3463398924815819618)
XLA Ops:
  0.6 0.0 copy-start
  0.6 1.1 %copy-done = bf16[24,128,1,128]{3,1,2,0:T(8,128)(2,1)S(1)} copy-done((bf16[24,128,1,128]{3,1,2,0:T(8,128)(2,1)S(1)}, bf16[24,128,1,128]{3,1,2,0:T(8,128)(2,1)}, u32[]{:S(2)}) %copy-start) | copy-done | bytes 786456
  1.8 0.0 copy-start.1
  1.8 0.0 copy-start.2
  1.8 0.0 copy-start.3
  1.8 0.5 %edge.1 = (bf16[48,128]{1,0:T(8,128)(2,1)S(1)}, bf16[48,128]{1,0:T(8,128)(2,1)S(1)}, bf16[256,128]{1,0:T(8,128)(2,1)S(1)}) custom-call(bf16[24,128,128]{2,1,0:T(8,128)(2,1)S(1)} %bitcast.11), custom_call_target="tpu_custom_call" | custom-call | flops 2000000000 | bytes 4000000 | tf_op jit(solution)/shard_map/edge/pallas_call | solution.py:276
  2.3 0.0 copy-start.6
  2.3 2.2 %collective-permute-start = (bf16[48,128]{1,0:T(8,128)(2,1)S(1)}, bf16[48,128]{1,0:T(8,128)(2,1)S(1)}, u32[]{:S(2)}, u32[]{:S(2)}) collective-permute-start(bf16[48,128]{1,0:T(8,128)(2,1)S(1)} %get-tuple-element.15), channel_id=1, source_target_pairs={{0,1},{1,2},{2,3},{3,0},{4,5},{5,6},{6,7},{7,4},{8,9},{9,10},{10,1... | collective-permute-start | bytes 36872 | tf_op jit(solution)/shard_map/ppermute | solution.py:290
  4.4 0.0 copy-start.4
  4.4 0.0 copy-start.5
  4.4 1.5 %collective-permute-start.1 = (bf16[48,128]{1,0:T(8,128)(2,1)S(1)}, bf16[48,128]{1,0:T(8,128)(2,1)S(1)}, u32[]{:S(2)}, u32[]{:S(2)}) collective-permute-start(bf16[48,128]{1,0:T(8,128)(2,1)S(1)} %get-tuple-element.16), channel_id=1, source_target_pairs={{1,0},{2,1},{3,2},{0,3},{5,4},{6,5},{7,6},{4,7},{9,8},{10,9},{11,1... | collective-permute-start | bytes 36872 | tf_op jit(solution)/shard_map/ppermute | solution.py:291
  6.0 0.0 copy-done.6
  6.0 0.0 copy-done.4
  6.0 0.0 copy-done.5
  6.0 0.0 copy-done.1
  6.0 0.0 copy-done.2
  6.0 0.0 copy-done.3
  6.0 2.0 %plan.1 = (bf16[8,256,128]{2,1,0:T(8,128)(2,1)S(1)}, bf16[128,128]{1,0:T(8,128)(2,1)S(1)}, bf16[2,8,16,128]{3,2,1,0:T(8,128)(2,1)S(1)}, f32[128,128]{1,0:T(8,128...) custom-call(bf16[24,128,128]{2,1,0:T(8,128)(2,1)S(1)} %bitcast.12, ...), custom_call_target="tpu_custom_call" | custom-call | flops 10000000 | bytes 1000000 | tf_op jit(solution)/shard_map/plan/pallas_call | solution.py:294
  8.1 0.0 collective-permute-done.before
  8.1 0.0 collective-permute-done.1.after
  8.1 1.0 %start.1 = f32[128,128]{1,0:T(8,128)} custom-call(bf16[48,128]{1,0:T(8,128)(2,1)S(1)} %collective-permute-done.before, bf16[48,128]{1,0:T(8,128)(2,1)S(1)} %collective-permute-done.1.after, bf16[128,256]{1,0:T(8,128)(2,1)S(1)} %get-tuple-element.23.picked_edge, bf16[128,128]{1,0:T(8,128)(2,1)S(1)} %get-tuple-element.24.reach_edge, ...), custom_call_target="tpu_custom_call" | custom-call | tf_op jit(solution)/shard_map/start/pallas_call | solution.py:319
  9.1 10.7 %all-to-all-start = ((f32[128,1,128]{2,1,0:T(1,128)}), f32[128,1,128]{2,1,0:T(1,128)S(1)}, u32[]{:S(2)}, u32[]{:S(2)}) async-start(f32[128,1,128]{2,1,0:T(1,128)} %bitcast.6), calls=%async_computation | async-start | bytes 131072 | tf_op jit(solution)/shard_map/all_to_all | solution.py:327
  19.8 5.2 %physics.1 = bf16[24,128,128]{2,1,0:T(8,128)(2,1)} custom-call(bf16[24,128,128]{2,1,0:T(8,128)(2,1)S(1)} %bitcast.13, bf16[48,128]{1,0:T(8,128)(2,1)S(1)} %collective-permute-done.before, bf16[48,128]{1,0:T(8,128)(2,1)S(1)} %collective-permute-done.1.after, bf16[128,128]{1,0:T(8,128)(2,1)S(1)} %get-tuple-element.18.near, ...), custom_call_target="tpu_custom_call" | custom-call | flops 10000000000 | bytes 10000000 | tf_op jit(solution)/shard_map/physics/pallas_call | solution.py:328
  25.0 4.4 %all-to-all-done = f32[128,1,128]{2,1,0:T(1,128)S(1)} async-done(((f32[128,1,128]{2,1,0:T(1,128)}), f32[128,1,128]{2,1,0:T(1,128)S(1)}, u32[]{:S(2)}, u32[]{:S(2)}) %all-to-all-start) | async-done | bytes 65568 | tf_op jit(solution)/shard_map/all_to_all | solution.py:327
  29.4 1.1 %order.1 = f32[24,128]{1,0:T(8,128)} custom-call(f32[128,128]{1,0:T(8,128)S(1)} %bitcast.14), custom_call_target="tpu_custom_call" | custom-call | tf_op jit(solution)/shard_map/order/pallas_call | solution.py:341
  (1 shorter events, 0.0 us)
Async XLA Ops:
  0.6 1.1 %copy-start = (bf16[24,128,1,128]{3,1,2,0:T(8,128)(2,1)S(1)}, bf16[24,128,1,128]{3,1,2,0:T(8,128)(2,1)}, u32[]{:S(2)}) copy-start(bf16[24,128,1,128]{3,1,2,0:T(8,128)(2,1)} %param.6) | copy-start | bytes 2359300
  1.8 4.3 %copy-start.1 = (bf16[24,128,1,128]{3,1,2,0:T(8,128)(2,1)S(1)}, bf16[24,128,1,128]{3,1,2,0:T(8,128)(2,1)}, u32[]{:S(2)}) copy-start(bf16[24,128,1,128]{3,1,2,0:T(8,128)(2,1)} %param.6) | copy-start | bytes 2359300
  1.8 4.3 %copy-start.2 = (bf16[8,128,128]{2,1,0:T(8,128)(2,1)S(1)}, bf16[8,128,128]{2,1,0:T(8,128)(2,1)}, u32[]{:S(2)}) copy-start(bf16[8,128,128]{2,1,0:T(8,128)(2,1)} %operators.1) | copy-start | bytes 786436
  1.8 4.3 %copy-start.3 = (bf16[128,1,128]{2,0,1:T(8,128)(2,1)S(1)}, bf16[128,1,128]{2,0,1:T(8,128)(2,1)}, u32[]{:S(2)}) copy-start(bf16[128,1,128]{2,0,1:T(8,128)(2,1)} %param.10) | copy-start | bytes 98308
  2.3 3.7 %copy-start.6 = (s32[4,1,128]{2,1,0:T(1,128)S(1)}, s32[4,1,128]{2,1,0:T(1,128)}, u32[]{:S(2)}) copy-start(s32[4,1,128]{2,1,0:T(1,128)} %param.7) | copy-start | bytes 6148
  2.3 5.8 %collective-permute-start = (bf16[48,128]{1,0:T(8,128)(2,1)S(1)}, bf16[48,128]{1,0:T(8,128)(2,1)S(1)}, u32[]{:S(2)}, u32[]{:S(2)}) collective-permute-start(bf16[48,128]{1,0:T(8,128)(2,1)S(1)} %get-tuple-element.15), channel_id=1, source_target_pairs={{0,1},{1,2},{2,3},{3,0},{4,5},{5,6},{6,7},{7,4},{8,9},{9,10},{10,1... | collective-permute-start | bytes 36872 | tf_op jit(solution)/shard_map/ppermute | solution.py:290
  4.4 1.5 %copy-start.4 = (s32[1,128]{1,0:T(1,128)S(1)}, s32[1,128]{1,0:T(1,128)}, u32[]{:S(2)}) copy-start(s32[1,128]{1,0:T(1,128)} %param.8) | copy-start | bytes 1540
  4.4 1.6 %copy-start.5 = (s32[1,128]{1,0:T(1,128)S(1)}, s32[1,128]{1,0:T(1,128)}, u32[]{:S(2)}) copy-start(s32[1,128]{1,0:T(1,128)} %param.9) | copy-start | bytes 1540
  4.4 3.6 %collective-permute-start.1 = (bf16[48,128]{1,0:T(8,128)(2,1)S(1)}, bf16[48,128]{1,0:T(8,128)(2,1)S(1)}, u32[]{:S(2)}, u32[]{:S(2)}) collective-permute-start(bf16[48,128]{1,0:T(8,128)(2,1)S(1)} %get-tuple-element.16), channel_id=1, source_target_pairs={{1,0},{2,1},{3,2},{0,3},{5,4},{6,5},{7,6},{4,7},{9,8},{10,9},{11,1... | collective-permute-start | bytes 36872 | tf_op jit(solution)/shard_map/ppermute | solution.py:291
  9.1 20.3 %all-to-all-start = ((f32[128,1,128]{2,1,0:T(1,128)}), f32[128,1,128]{2,1,0:T(1,128)S(1)}, u32[]{:S(2)}, u32[]{:S(2)}) async-start(f32[128,1,128]{2,1,0:T(1,128)} %bitcast.6), calls=%async_computation | async-start | bytes 131072 | tf_op jit(solution)/shard_map/all_to_all | solution.py:327
